TPU v7x, 128 devices: a whole 4x4x4 slice. The times are simulated.
128 devices in a mesh: ingest: 16 (over y, x), gr: 4 (over z), gc: 2 (over core).
Axes of the slice: x: 4, y: 4, z: 4, core: 2. Of those that a mesh axis runs over, the one named last changes fastest.
Arguments:
- embeddings: bfloat16 [131072, 768], P('ingest'), may hold values from -12 to 12
- cluster_ids: int32 [131072, 1], P('ingest'), may hold values from 0 to 127, as said below
- cluster_slots: int32 [128], replicated, may hold values from 0 to 127, each once
Outputs:
- mean_rows: bfloat16 [128, 2048, 768], P('ingest', 'gr', 'gc')
- dup_score: float32 [128, 2048], P('ingest', 'gr')
Inputs may be any that keep to these rules, and one draw needn't show every extreme that they name: `cluster_ids`: within each shard of 8192 rows at most 128 rows fall in one cluster; one cluster has exactly 128 rows in every shard.
All inputs are finite; a program needn't handle non-finite values.
Results may differ from a plain program's by a relative error of at most 0.0034.
Values may be sent and summed in bfloat16 or wider, within the bound.
No kernel may reach another device: no remote copies, remote signals or barrier semaphores. Data moves between devices by JAX's collectives and lax.ppermute only.
A program may use at most 128 MiB of HBM per device.

v0:
```python
import jax
import jax.numpy as jnp
from jax import lax
from jax.sharding import PartitionSpec as P

D = 768
PER_SRC = 128
CLUS_MEM = 1


sharpness = 8.0
epsilon = 1e-06


def normalize(cluster_rows):
    widened = cluster_rows.astype(jnp.float32)
    squares = jnp.sum(widened * widened, axis=-1, keepdims=True)
    return (widened * lax.rsqrt(squares + epsilon)).astype(jnp.bfloat16)


def whole_cluster(members):
    rows_data, normed_all, occupied_all = members
    capacity = rows_data.shape[0]
    width = rows_data.shape[1]
    block_rows = min(512, capacity)
    block_count = capacity // block_rows

    def one_block(pair):
        normed_block, occupied_block = pair
        cosine = jnp.dot(normed_block, normed_all.T, preferred_element_type=jnp.float32)
        weights = (
            occupied_block[:, None] * occupied_all[None, :] * jnp.exp(sharpness * (cosine - 1.0))
        )
        totals = jnp.sum(weights, axis=1)
        summed = jnp.dot(
            weights.astype(jnp.bfloat16), rows_data, preferred_element_type=jnp.float32
        )
        divisor = totals + 1.0 - occupied_block
        return ((summed / divisor[:, None]).astype(jnp.bfloat16), jnp.log(divisor))

    means, scores = lax.map(
        one_block,
        (
            normed_all.reshape(block_count, block_rows, width),
            occupied_all.reshape(block_count, block_rows),
        ),
    )
    return (means.reshape(capacity, width), scores.reshape(capacity))


def on_device(embeddings, cluster_ids, cluster_slots):
    sources = lax.axis_size("ingest")
    grid_rows = lax.axis_size("gr")
    grid_cols = lax.axis_size("gc")
    group_size = grid_rows * grid_cols
    clusters = cluster_slots.shape[0]
    owned_count = clusters // sources
    capacity = sources * PER_SRC
    member = lax.axis_index("gr") * grid_cols + lax.axis_index("gc")
    cluster_of = cluster_ids[:, 0]
    onehot = (cluster_of[:, None] == jnp.arange(clusters, dtype=jnp.int32)[None, :]).astype(
        jnp.int32
    )
    row_rank = jnp.sum(jnp.cumsum(onehot, axis=0) * onehot, axis=1) - 1
    counts = jnp.sum(onehot, axis=0)
    slot_of = jnp.sum(onehot * cluster_slots[None, :], axis=1)
    target = slot_of // owned_count
    within = slot_of % owned_count
    slot_counts = jnp.zeros((clusters,), jnp.int32).at[cluster_slots].set(counts)
    slot_counts = slot_counts.reshape(sources, owned_count).T.astype(jnp.bfloat16)
    total_slots = CLUS_MEM * sources * PER_SRC
    mine = within // CLUS_MEM == member
    local_position = ((within - member * CLUS_MEM) * sources + target) * PER_SRC + row_rank
    local_position = jnp.where(mine, local_position, total_slots)
    outgoing = (
        jnp.zeros((total_slots, D), jnp.bfloat16).at[local_position].set(embeddings, mode="drop")
    )
    outgoing = outgoing.reshape(CLUS_MEM, sources, PER_SRC, D)
    counts_mine = lax.dynamic_slice_in_dim(slot_counts, member * CLUS_MEM, CLUS_MEM, 0)
    arrived, arrived_counts = (
        lax.all_to_all(outgoing, "ingest", split_axis=1, concat_axis=1, tiled=True),
        lax.all_to_all(counts_mine, "ingest", split_axis=1, concat_axis=1, tiled=True),
    )
    cluster_rows = arrived.reshape(CLUS_MEM, capacity, D)
    occupied = (
        jnp.arange(PER_SRC, dtype=jnp.int32)[None, None, :].astype(jnp.float32)
        < arrived_counts.astype(jnp.float32)[:, :, None]
    )
    occupied = occupied.reshape(CLUS_MEM, capacity).astype(jnp.float32)
    normed = normalize(cluster_rows)
    means, scores = lax.map(whole_cluster, (cluster_rows, normed, occupied))
    row_span = capacity // grid_rows
    feature_span = D // grid_cols
    tiles = means.reshape(CLUS_MEM, grid_rows, row_span, grid_cols, feature_span)
    tiles = tiles.transpose(1, 3, 0, 2, 4).reshape(group_size, CLUS_MEM, row_span, feature_span)
    score_tiles = scores.reshape(CLUS_MEM, grid_rows, row_span).transpose(1, 0, 2)
    score_tiles = jnp.broadcast_to(score_tiles[:, None], (grid_rows, grid_cols, CLUS_MEM, row_span))
    score_tiles = score_tiles.reshape(group_size, CLUS_MEM, row_span)
    mean_rows = lax.all_to_all(
        tiles, ("gr", "gc"), split_axis=0, concat_axis=0, tiled=True
    ).reshape(owned_count, row_span, feature_span)
    dup_score = lax.all_to_all(
        score_tiles, ("gr", "gc"), split_axis=0, concat_axis=0, tiled=True
    ).reshape(owned_count, row_span)
    return (mean_rows, dup_score)


def solution(mesh):
    return jax.shard_map(
        on_device,
        mesh=mesh,
        in_specs=(P("ingest", None), P("ingest", None), P()),
        out_specs=(P("ingest", "gr", "gc"), P("ingest", "gr")),
        check_vma=False,
    )
```

profile of v0, /device:TPU:1, one launch (start us, length us, event | category | flops | bytes accessed | tf_op | source)
XLA Modules:
  0.0 220.5 jit_solution(13703302360913041915)
XLA Ops:
  3.3 1.9 copy-done
  5.3 2.6 %broadcast_add_fusion.1 = s32[128,64,128]{0,1,2:T(8,128)S(1)} fusion(s32[128,64,128]{0,1,2:T(8,128)} %copy-done, s32[128,64]{0,1:T(8,128)S(1)} %slice.9), kind=kLoop, calls=%fused_computation.29 | loop fusion | flops 1048576 | bytes 8421376 | tf_op jit(solution)/shard_map/reduce_window_sum
  8.0 2.4 %copy.17 = s32[128,64,128]{0,2,1:T(8,128)S(1)} copy(s32[128,64,128]{0,1,2:T(8,128)S(1)} %broadcast_add_fusion.1) | data formatting | bytes 8388608 | tf_op jit(solution)/shard_map/reduce_window_sum
  10.4 4.2 %select_reduce_fusion = (s32[8192]{0:T(1024)S(1)}, s32[8192]{0:T(1024)S(1)}, s32[128]{0:T(128)S(1)}) fusion(s32[128]{0:T(128)S(1)} %copy-done.2, s32[8192]{0:T(1024)S(1)} %bitcast.81, s32[128,64,128]{0,2,1:T(8,128)S(1)} %copy.17), kind=kLoop, calls=%fused_computation.26 | loop fusion | flops 7323520 | bytes 4293632 | tf_op jit(solution)/shard_map/reduce_sum | solution.py:66
  16.6 7.6 %all-to-all-start = ((bf16[1,16,1]{2,0,1:T(2,128)(2,1)}), bf16[1,16,1]{2,0,1:T(2,128)(2,1)S(1)}, u32[]{:S(2)}, u32[]{:S(2)}) async-start(bf16[1,16,1]{2,0,1:T(2,128)(2,1)} %all_to_all.20), calls=%async_computation | async-start | bytes 16384 | tf_op jit(solution)/shard_map/all_to_all | solution.py:82
  24.5 38.7 %scatter_custom_fusion.1 = bf16[2048,768]{1,0:T(8,128)(2,1)} fusion(s32[8192]{0:T(1024)S(1)} %bitcast.84, bf16[8192,768]{1,0:T(8,128)(2,1)} %param.5, bf16[]{:T(256)} %constant.118.clone.1), kind=kCustom, calls=%fused_computation.31 | custom fusion | bytes 3146240 | tf_op jit(solution)/shard_map/scatter | solution.py:76
  63.2 6.7 %all-to-all-start.1 = ((bf16[1,16,128,768]{3,2,0,1:T(8,128)(2,1)}), bf16[1,16,128,768]{3,2,0,1:T(8,128)(2,1)S(1)}, u32[]{:S(2)}, u32[]{:S(2)}) async-start(bf16[1,16,128,768]{3,2,0,1:T(8,128)(2,1)} %bitcast.74), calls=%async_computation.1 | async-start | bytes 6291456 | tf_op jit(solution)/shard_map/all_to_all | solution.py:81
  70.2 45.0 %all-to-all-done.1 = bf16[1,16,128,768]{3,2,0,1:T(8,128)(2,1)S(1)} async-done(((bf16[1,16,128,768]{3,2,0,1:T(8,128)(2,1)}), bf16[1,16,128,768]{3,2,0,1:T(8,128)(2,1)S(1)}, u32[]{:S(2)}, u32[]{:S(2)}) %all-to-all-start.1) | async-done | bytes 3145760 | tf_op jit(solution)/shard_map/all_to_all | solution.py:81
  115.9 2.2 %multiply_convert_fusion.1 = bf16[4,512,768]{2,1,0:T(8,128)(2,1)} fusion(f32[4,512]{1,0:T(4,128)S(1)} %rsqrt.16, bf16[4,512,768]{2,1,0:T(8,128)(2,1)S(1)} %bitcast.72), kind=kLoop, calls=%fused_computation.19 | loop fusion | flops 4718592 | bytes 6299648 | tf_op jit(solution)/shard_map/convert_element_type | solution.py:18
  118.2 2.3 %multiply_convert_fusion = bf16[2048,768]{1,0:T(8,128)(2,1)} fusion(f32[2048]{0:T(1024)S(1)} %get-tuple-element.171, bf16[1,16,128,768]{3,2,0,1:T(8,128)(2,1)S(1)} %all-to-all-done.1), kind=kLoop, calls=%fused_computation.18 | loop fusion | flops 4718592 | bytes 6299648 | tf_op jit(solution)/shard_map/convert_element_type | solution.py:18
  120.5 39.9 %while.24 = (s32[]{:T(128)}, bf16[4,512,768]{2,1,0:T(8,128)(2,1)}, f32[4,512]{1,0:T(4,128)S(1)}, f32[4,512]{1,0:T(4,128)S(1)}, bf16[4,512,768]{2,1,0:T(8,128)(2,...) while((s32[]{:T(128)}, bf16[4,512,768]{2,1,0:T(8,128)(2,1)}, ...), condition=%wide.region_10.11_spmd.clone, body=%wide.region_8.10_spmd.clone.sunk | while | flops 3228308480 | bytes 12120777 | solution.py:41
  120.6 5.5 %fusion.40 = (f32[512]{0:T(512)S(1)}, bf16[512,2048]{1,0:T(8,128)(2,1)}) fusion(bf16[2048,768]{1,0:T(8,128)(2,1)} %get-tuple-element.265, bf16[4,512,768]{2,1,0:T(8,128)(2,1)} %get-tuple-element.264, s32[]{:T(128)S(6)} %copy.28, f32[2048]{0:T(1024)S(1)} %fusion.39, f32[512]{0:T(512)S(1)} %bitcast.77), kind=kOutput, calls=%fused_computation.53.clone.1 | convolution fusion | flops 1616903680 | bytes 6041604 | tf_op jit(solution)/shard_map/while/body/eval_jaxpr/while/body/eval_jaxpr/dot_general | solution.py:30
  126.2 4.3 %fusion.41 = bf16[4,512,768]{2,1,0:T(8,128)(2,1)} fusion(bf16[4,512,768]{2,1,0:T(8,128)(2,1)} %get-tuple-element.250, s32[]{:T(128)S(6)} %copy.28, bf16[2048,768]{1,0:T(8,128)(2,1)S(1)} %get-tuple-element.266, bf16[512,2048]{1,0:T(8,128)(2,1)} %get-tuple-element.234, f32[512]{0:T(512)S(1)} %get-tuple-element.236), kind=kOutput, calls=%fused_computation.8.clone.1 | convolution fusion | flops 1611399168 | bytes 6031364 | tf_op jit(solution)/shard_map/while/body/eval_jaxpr/while/body/eval_jaxpr/dot_general | solution.py:35
  130.5 5.5 %fusion.40 = (f32[512]{0:T(512)S(1)}, bf16[512,2048]{1,0:T(8,128)(2,1)}) fusion(bf16[2048,768]{1,0:T(8,128)(2,1)} %get-tuple-element.265, bf16[4,512,768]{2,1,0:T(8,128)(2,1)} %get-tuple-element.264, s32[]{:T(128)S(6)} %copy.28, f32[2048]{0:T(1024)S(1)} %fusion.39, f32[512]{0:T(512)S(1)} %bitcast.77), kind=kOutput, calls=%fused_computation.53.clone.1 | convolution fusion | flops 1616903680 | bytes 6041604 | tf_op jit(solution)/shard_map/while/body/eval_jaxpr/while/body/eval_jaxpr/dot_general | solution.py:30
  136.1 4.3 %fusion.41 = bf16[4,512,768]{2,1,0:T(8,128)(2,1)} fusion(bf16[4,512,768]{2,1,0:T(8,128)(2,1)} %get-tuple-element.250, s32[]{:T(128)S(6)} %copy.28, bf16[2048,768]{1,0:T(8,128)(2,1)S(1)} %get-tuple-element.266, bf16[512,2048]{1,0:T(8,128)(2,1)} %get-tuple-element.234, f32[512]{0:T(512)S(1)} %get-tuple-element.236), kind=kOutput, calls=%fused_computation.8.clone.1 | convolution fusion | flops 1611399168 | bytes 6031364 | tf_op jit(solution)/shard_map/while/body/eval_jaxpr/while/body/eval_jaxpr/dot_general | solution.py:35
  140.5 5.5 %fusion.40 = (f32[512]{0:T(512)S(1)}, bf16[512,2048]{1,0:T(8,128)(2,1)}) fusion(bf16[2048,768]{1,0:T(8,128)(2,1)} %get-tuple-element.265, bf16[4,512,768]{2,1,0:T(8,128)(2,1)} %get-tuple-element.264, s32[]{:T(128)S(6)} %copy.28, f32[2048]{0:T(1024)S(1)} %fusion.39, f32[512]{0:T(512)S(1)} %bitcast.77), kind=kOutput, calls=%fused_computation.53.clone.1 | convolution fusion | flops 1616903680 | bytes 6041604 | tf_op jit(solution)/shard_map/while/body/eval_jaxpr/while/body/eval_jaxpr/dot_general | solution.py:30
  146.1 4.3 %fusion.41 = bf16[4,512,768]{2,1,0:T(8,128)(2,1)} fusion(bf16[4,512,768]{2,1,0:T(8,128)(2,1)} %get-tuple-element.250, s32[]{:T(128)S(6)} %copy.28, bf16[2048,768]{1,0:T(8,128)(2,1)S(1)} %get-tuple-element.266, bf16[512,2048]{1,0:T(8,128)(2,1)} %get-tuple-element.234, f32[512]{0:T(512)S(1)} %get-tuple-element.236), kind=kOutput, calls=%fused_computation.8.clone.1 | convolution fusion | flops 1611399168 | bytes 6031364 | tf_op jit(solution)/shard_map/while/body/eval_jaxpr/while/body/eval_jaxpr/dot_general | solution.py:35
  150.5 5.5 %fusion.40 = (f32[512]{0:T(512)S(1)}, bf16[512,2048]{1,0:T(8,128)(2,1)}) fusion(bf16[2048,768]{1,0:T(8,128)(2,1)} %get-tuple-element.265, bf16[4,512,768]{2,1,0:T(8,128)(2,1)} %get-tuple-element.264, s32[]{:T(128)S(6)} %copy.28, f32[2048]{0:T(1024)S(1)} %fusion.39, f32[512]{0:T(512)S(1)} %bitcast.77), kind=kOutput, calls=%fused_computation.53.clone.1 | convolution fusion | flops 1616903680 | bytes 6041604 | tf_op jit(solution)/shard_map/while/body/eval_jaxpr/while/body/eval_jaxpr/dot_general | solution.py:30
  156.1 4.3 %fusion.41 = bf16[4,512,768]{2,1,0:T(8,128)(2,1)} fusion(bf16[4,512,768]{2,1,0:T(8,128)(2,1)} %get-tuple-element.250, s32[]{:T(128)S(6)} %copy.28, bf16[2048,768]{1,0:T(8,128)(2,1)S(1)} %get-tuple-element.266, bf16[512,2048]{1,0:T(8,128)(2,1)} %get-tuple-element.234, f32[512]{0:T(512)S(1)} %get-tuple-element.236), kind=kOutput, calls=%fused_computation.8.clone.1 | convolution fusion | flops 1611399168 | bytes 6031364 | tf_op jit(solution)/shard_map/while/body/eval_jaxpr/while/body/eval_jaxpr/dot_general | solution.py:35
  161.0 7.6 %all-to-all-start.3 = ((f32[8,1,512]{2,1,0:T(1,128)}), f32[8,1,512]{2,1,0:T(1,128)S(1)}, u32[]{:S(2)}, u32[]{:S(2)}) async-start(f32[8,1,512]{2,1,0:T(1,128)} %broadcast_in_dim.47), calls=%async_computation.3 | async-start | bytes 32768 | tf_op jit(solution)/shard_map/all_to_all | solution.py:102
  168.6 5.8 %reshape.282 = bf16[1,4,512,2,384]{4,3,2,1,0:T(2,128)(2,1)S(1)} reshape(bf16[4,512,768]{2,1,0:T(8,128)(2,1)} %get-tuple-element.122) | data formatting | bytes 6291456 | tf_op jit(solution)/shard_map/reshape | solution.py:94
  174.5 2.1 copy.19
  176.6 4.8 %all-to-all-start.2 = ((bf16[8,1,512,384]{3,2,1,0:T(8,128)(2,1)}), bf16[8,1,512,384]{3,2,1,0:T(8,128)(2,1)S(1)}, u32[]{:S(2)}, u32[]{:S(2)}) async-start(bf16[8,1,512,384]{3,2,1,0:T(8,128)(2,1)} %bitcast.15), calls=%async_computation.2 | async-start | bytes 6291456 | tf_op jit(solution)/shard_map/all_to_all | solution.py:99
  182.0 36.8 %all-to-all-done.2 = bf16[8,1,512,384]{3,2,1,0:T(8,128)(2,1)S(1)} async-done(((bf16[8,1,512,384]{3,2,1,0:T(8,128)(2,1)}), bf16[8,1,512,384]{3,2,1,0:T(8,128)(2,1)S(1)}, u32[]{:S(2)}, u32[]{:S(2)}) %all-to-all-start.2) | async-done | bytes 3145760 | tf_op jit(solution)/shard_map/all_to_all | solution.py:99
  (59 shorter events, 9.6 us)
Async XLA Ops:
  3.3 1.9 copy-start
  8.0 2.5 %copy-start.1 = (s32[8192,1]{0,1:T(1,128)S(1)}, s32[8192,1]{0,1:T(1,128)}, u32[]{:S(2)}) copy-start(s32[8192,1]{0,1:T(1,128)} %param.6) | copy-start | bytes 98308
  8.0 2.5 %copy-start.2 = (s32[128]{0:T(128)S(1)}, s32[128]{0:T(128)}, u32[]{:S(2)}) copy-start(s32[128]{0:T(128)} %param.7) | copy-start | bytes 1540
  16.6 46.6 %all-to-all-start = ((bf16[1,16,1]{2,0,1:T(2,128)(2,1)}), bf16[1,16,1]{2,0,1:T(2,128)(2,1)S(1)}, u32[]{:S(2)}, u32[]{:S(2)}) async-start(bf16[1,16,1]{2,0,1:T(2,128)(2,1)} %all_to_all.20), calls=%async_computation | async-start | bytes 16384 | tf_op jit(solution)/shard_map/all_to_all | solution.py:82
  63.2 52.0 %all-to-all-start.1 = ((bf16[1,16,128,768]{3,2,0,1:T(8,128)(2,1)}), bf16[1,16,128,768]{3,2,0,1:T(8,128)(2,1)S(1)}, u32[]{:S(2)}, u32[]{:S(2)}) async-start(bf16[1,16,128,768]{3,2,0,1:T(8,128)(2,1)} %bitcast.74), calls=%async_computation.1 | async-start | bytes 6291456 | tf_op jit(solution)/shard_map/all_to_all | solution.py:81
  161.0 15.6 %all-to-all-start.3 = ((f32[8,1,512]{2,1,0:T(1,128)}), f32[8,1,512]{2,1,0:T(1,128)S(1)}, u32[]{:S(2)}, u32[]{:S(2)}) async-start(f32[8,1,512]{2,1,0:T(1,128)} %broadcast_in_dim.47), calls=%async_computation.3 | async-start | bytes 32768 | tf_op jit(solution)/shard_map/all_to_all | solution.py:102
  176.6 42.2 %all-to-all-start.2 = ((bf16[8,1,512,384]{3,2,1,0:T(8,128)(2,1)}), bf16[8,1,512,384]{3,2,1,0:T(8,128)(2,1)S(1)}, u32[]{:S(2)}, u32[]{:S(2)}) async-start(bf16[8,1,512,384]{3,2,1,0:T(8,128)(2,1)} %bitcast.15), calls=%async_computation.2 | async-start | bytes 6291456 | tf_op jit(solution)/shard_map/all_to_all | solution.py:99
where the time goes:
time: 221 us; the launch traced here: 220 us
  waiting for transfers between devices  81.8 us (37%)
  local copies, waits for them, and re-layouts  57.3 us (26%)
  matrix products  39.2 us (18%)
  starting transfers between devices  26.7 us (12%)
  other arithmetic  14.6 us (7%)
    all_to_all x1, waiting for transfers between devices, on_device(): lax.all_to_all(outgoing, 'ingest', split_axis=1, concat_axis=1, tiled=True)  45 us
    scatter x1, local copies, waits for them, and re-layouts, on_device(): jnp.zeros((total_slots, D), jnp.bfloat16).at[local_position]  38.7 us
    all_to_all x1, waiting for transfers between devices, on_device(): lax.all_to_all(tiles, ('gr', 'gc'), split_axis=0, concat_axis=0, tiled=True)  36.8 us
    dot_general x4, matrix products, one_block(): jnp.dot(normed_block, normed_all.T, preferred_element_type=jnp.float32)  22.1 us
    dot_general x4, matrix products, one_block(): jnp.dot(weights.astype(jnp.bfloat16), rows_data, preferred_element_type=j...  17.1 us
    reshape x2, local copies, waits for them, and re-layouts, on_device(): means.reshape(CLUS_MEM, grid_rows, row_span, grid_cols, feature_span)  7.92 us
    all_to_all x1, starting transfers between devices, on_device(): lax.all_to_all(score_tiles, ('gr', 'gc'), split_axis=0, concat_axis=0, ti...  7.64 us
    all_to_all x1, starting transfers between devices, on_device(): lax.all_to_all(counts_mine, 'ingest', split_axis=1, concat_axis=1, tiled=...  7.57 us
  transfers between devices with their start and end apart: 4, of which 2 were waited for; matrix products, arithmetic and copies ran while one was open for 22% of the time, Pallas kernels for 0%

commit v1 on v0

v1 whole, which is shorter than its diff:
```python
import functools
import jax
import jax.numpy as jnp
from jax import lax
from jax.experimental import pallas as pl
from jax.experimental.pallas import tpu as pltpu
from jax.sharding import PartitionSpec as P

D = 768
NT=(((1,),(1,)),((),()))
NN=(((1,),(0,)),((),()))
bf16=jnp.bfloat16; f32=jnp.float32
ROWS=8192; CH=ROWS//128; NSEG=8; W=64; CPAD=2048+W
def dot(a,b,dn=NN): return lax.dot_general(a,b,dn,preferred_element_type=f32)
def iota(shape,d): return lax.broadcasted_iota(jnp.int32,shape,d)
def gk(par, ids_ref, slots_ref, emb_ref, out_ref, C, emb_v, ev, rt, gref, base_v, base_s, inv_s, sem, dsem, *, NK, PR):
    NG=16*NK
    seg=ROWS//NSEG
    cps=[pltpu.make_async_copy(emb_ref.at[pl.ds(s*seg,seg)],emb_v.at[pl.ds(s*seg,seg)],sem.at[s]) for s in range(NSEG)]
    for c in cps: c.start()
    C[...]=jnp.zeros_like(C)
    gi=iota((NG,128),0)
    want=(gi%16)*8+par[0]+gi//16
    cl=jnp.sum(jnp.where(slots_ref[...]==want,iota((NG,128),1),0),axis=1,keepdims=True)
    ids=ids_ref[...]
    E=(ids[:,None,:]==cl[None,:,:]).astype(f32)
    Eb=E.astype(bf16).reshape(CH*NG,128)
    U=(iota((128,128),0)<iota((128,128),1)).astype(bf16)
    ONE=jnp.ones((128,128),bf16)
    pre=dot(Eb,U).reshape(CH,NG,128)
    tot=dot(Eb,ONE).reshape(CH,NG,128)
    roff=par[1].astype(f32)
    carry=jnp.zeros((NG,128),f32)-roff
    ranks=[];vals=[];hotv=[]
    for a in range(CH):
        r=carry+pre[a]
        carry=carry+tot[a]
        e=E[a]
        v=jnp.where((r>=0)&(r<PR),e,0.0)
        hotv.append(v)
        ranks.append(jnp.sum(v*(r+1.0),axis=0,keepdims=True)-1.0)
        vals.append(jnp.sum(v,axis=0,keepdims=True))
    rank_row=jnp.concatenate(ranks,axis=0)
    vrow=jnp.concatenate(vals,axis=0)
    vb=vrow.astype(bf16)
    pg=dot(vb,U)
    tb=dot(vb,ONE).astype(bf16)
    L=(iota((CH,CH),1)<iota((CH,CH),0)).astype(bf16)
    g=dot(L,tb)+pg
    gref[...]=jnp.where(vrow>0,g,-1e6).astype(jnp.int32)
    trow=dot(jnp.ones((8,128),bf16),vb,NT).astype(bf16)
    UC=(iota((CH,128),0)<iota((CH,128),1)).astype(bf16)
    base_v[...]=dot(trow,UC).astype(jnp.int32)
    cp=pltpu.make_async_copy(base_v,base_s,dsem)
    cp.start()
    val=g+1.0
    hi=jnp.floor(val*(1.0/64.0)); lo=val-64.0*hi
    pi=iota((PR,128),0).astype(f32)
    for a in range(CH):
        rt[:,a*128:(a+1)*128]=(rank_row[a:a+1]==pi).astype(bf16)
        ev[0:NG,a*128:(a+1)*128]=(hotv[a]*hi[a:a+1]).astype(bf16)
        ev[NG:2*NG,a*128:(a+1)*128]=(hotv[a]*lo[a:a+1]).astype(bf16)
    hl=dot(rt[...],ev[...],NT)
    inv_s[...]=64.0*hl[:,:NG]+hl[:,NG:]-1.0
    cp.wait()
    ji=iota((W,256),0)
    cps_per=seg//256
    for s in range(NSEG):
        cps[s].wait()
        def body(i,_):
            b0=base_s[0,2*i]; b1=base_s[0,2*i+2]
            al=(b0//16)*16
            nw=jnp.where(b1>b0,(b1-al+W-1)//W,0)
            gr=jnp.concatenate([gref[pl.ds(2*i,1),:],gref[pl.ds(2*i+1,1),:]],axis=1)
            x=emb_v[pl.ds(pl.multiple_of(i*256,256),256),:]
            def win(w,_):
                st=pl.multiple_of(al+w*W,16)
                p=((gr-st)==ji).astype(f32).astype(bf16)
                y=dot(p,x).astype(bf16)
                C[pl.ds(st,W),:]=C[pl.ds(st,W),:]+y
                return 0
            lax.fori_loop(0,nw,win,0)
            return 0
        lax.fori_loop(s*cps_per,(s+1)*cps_per,body,0)
    nm=base_s[0,CH]
    GB=256//PR
    def perm(K):
        def tile(n,_):
            cols=[]
            for u in range(GB):
                cols.append(jnp.sum(jnp.where(iota((PR,NG),1)==n*GB+u,inv_s[...],0.0),axis=1,keepdims=True))
            col=jnp.concatenate(cols,axis=0)
            ki=iota((256,K),1).astype(f32)
            p=(col==ki).astype(bf16)
            y=dot(p,C[0:K,:])
            o=pl.multiple_of(n*256,256)
            out_ref[pl.ds(o,256),:]=y.astype(bf16)
            h=y[:,0:128]+jnp.where((col<0.0)&(iota((256,128),1)==0),64.0,0.0)
            out_ref[pl.ds(o,256),0:128]=h.astype(bf16)
            return 0
        lax.fori_loop(0,NG//GB,tile,0)
    @pl.when(nm<=1280)
    def _(): perm(1280)
    @pl.when(nm>1280)
    def _(): perm(2048)
def gather(par,ids,slots,emb,NK,PR):
    NG=16*NK
    return pl.pallas_call(functools.partial(gk,NK=NK,PR=PR),
      in_specs=[pl.BlockSpec(memory_space=pltpu.SMEM),pl.BlockSpec(memory_space=pltpu.VMEM),pl.BlockSpec(memory_space=pltpu.VMEM),pl.BlockSpec(memory_space=pl.ANY)],
      out_specs=pl.BlockSpec(memory_space=pltpu.VMEM),
      out_shape=jax.ShapeDtypeStruct((NG*PR,D),bf16),
      scratch_shapes=[pltpu.VMEM((CPAD,D),bf16),pltpu.VMEM((ROWS,D),bf16),pltpu.VMEM((2*NG,ROWS),bf16),pltpu.VMEM((PR,ROWS),bf16),
        pltpu.VMEM((CH,128),jnp.int32),pltpu.VMEM((8,128),jnp.int32),pltpu.SMEM((8,128),jnp.int32),pltpu.VMEM((PR,NG),f32),
        pltpu.SemaphoreType.DMA((NSEG,)),pltpu.SemaphoreType.DMA],
      compiler_params=pltpu.CompilerParams(vmem_limit_bytes=60<<20),
      )(par,ids.reshape(CH,128),slots.reshape(1,128),emb)
CAP = 2048
LOG2E = 1.4426950408889634


def ck(x_ref, out_ref, sc_ref, normed, bias, *, bq):
    i = pl.program_id(0)

    @pl.when(i == 0)
    def _():
        for k in range(CAP // 256):
            s = pl.ds(k * 256, 256)
            v = x_ref[s, :].astype(f32)
            sq = jnp.sum(v * v, axis=1, keepdims=True)
            normed[s, :] = (v * lax.rsqrt(sq + 1e-6)).astype(bf16)
        e0 = (iota((8, D), 1) == 0).astype(bf16)
        f0 = dot(e0, x_ref[...], NT)
        bias[...] = jnp.where(f0 > 32.0, -1e30, -8.0 * LOG2E)

    q = normed[pl.ds(i * bq, bq), :]
    cos = dot(q, normed[...], NT)
    w = jnp.exp2(cos * (8.0 * LOG2E) + bias[0:1, :])
    tot = jnp.sum(w, axis=1, keepdims=True)
    nb = dot(w.astype(bf16), x_ref[...])
    un = x_ref[pl.ds(i * bq, bq), 0:1].astype(f32) > 32.0
    div = jnp.where(un, 1.0, tot)
    m = jnp.where(un, 0.0, nb / div).astype(bf16)
    out_ref[0, 0] = m[:, :384]
    out_ref[0, 1] = m[:, 384:]
    sc_ref[...] = jnp.broadcast_to(jnp.log(div), (bq, 128)).T[0:1, :].reshape(1, 1, bq)


def cluster(x, bq=512):
    n = CAP // bq
    per = 512 // bq
    return pl.pallas_call(
        functools.partial(ck, bq=bq),
        grid=(n,),
        in_specs=[pl.BlockSpec((CAP, D), lambda i: (0, 0))],
        out_specs=[
            pl.BlockSpec((1, 2, bq, 384), lambda i: (i // per, 0, i % per, 0)),
            pl.BlockSpec((1, 1, bq), lambda i: (i, 0, 0)),
        ],
        out_shape=[
            jax.ShapeDtypeStruct((4, 2, 512, 384), bf16),
            jax.ShapeDtypeStruct((n, 1, bq), f32),
        ],
        scratch_shapes=[pltpu.VMEM((CAP, D), bf16), pltpu.VMEM((8, CAP), f32)],
        compiler_params=pltpu.CompilerParams(vmem_limit_bytes=60 << 20),
        cost_estimate=pl.CostEstimate(
            flops=4 * CAP * CAP * D, bytes_accessed=4 * CAP * D, transcendentals=CAP * CAP
        ),
    )(x)


def on_device(embeddings, cluster_ids, cluster_slots):
    member = lax.axis_index("gr") * 2 + lax.axis_index("gc")
    par = jnp.stack([member, member * 0]).astype(jnp.int32)
    outgoing = gather(par, cluster_ids, cluster_slots, embeddings, 1, 128)
    arrived = lax.all_to_all(
        outgoing.reshape(16, 128, D), "ingest", split_axis=0, concat_axis=0, tiled=True
    )
    means, scores = cluster(arrived.reshape(CAP, D))
    tiles = means.reshape(8, 1, 512, 384)
    score_tiles = jnp.broadcast_to(scores.reshape(4, 1, 1, 512), (4, 2, 1, 512)).reshape(8, 1, 512)
    mean_rows = lax.all_to_all(tiles, ("gr", "gc"), split_axis=0, concat_axis=0, tiled=True)
    dup_score = lax.all_to_all(score_tiles, ("gr", "gc"), split_axis=0, concat_axis=0, tiled=True)
    return (mean_rows.reshape(8, 512, 384), dup_score.reshape(8, 512))


def solution(mesh):
    return jax.shard_map(
        on_device,
        mesh=mesh,
        in_specs=(P("ingest", None), P("ingest", None), P()),
        out_specs=(P("ingest", "gr", "gc"), P("ingest", "gr")),
        check_vma=False,
    )
```

time: 221 us -> 141 us (0.64)
  blocking collectives: 0 us -> 58.9 us
  local copies, waits for them, and re-layouts: 57.3 us -> 3.01 us
  waiting for transfers between devices: 81.8 us -> 36.9 us
  matrix products: 39.2 us -> 0 us
  Pallas kernels: 0 us -> 37 us
  starting transfers between devices: 26.7 us -> 4.26 us
  other arithmetic: 14.6 us -> 0.65 us
    all_to_all x0 -> x2, blocking collectives: none -> 58.9 us  [the longest x1 46.2 us: on_device(): lax.all_to_all(outgoing.reshape(16, 128, D), 'ingest', split_axis=0, conc...]
    all_to_all x3 -> x0, waiting for transfers between devices: 45 us -> none  [the longest x1 45 us: on_device(): lax.all_to_all(outgoing, 'ingest', split_axis=1, concat_axis=1, tiled=True)]
    scatter x2 -> x0, local copies, waits for them, and re-layouts: 39.6 us -> none  [the longest x1 38.7 us: on_device(): jnp.zeros((total_slots, D), jnp.bfloat16).at[local_position]]
    dot_general x8 -> x0, matrix products: 39.2 us -> none  [the longest x4 22.1 us: one_block(): jnp.dot(normed_block, normed_all.T, preferred_element_type=jnp.float32)]
    pallas_call x0 -> x2, Pallas kernels: none -> 37 us  [the longest x1 18.7 us: cluster(): pl.pallas_call(functools.partial(ck, bq=bq), grid=(n,), in_specs=[pl.Bloc...]
    all_to_all x3 -> x0, starting transfers between devices: 21.9 us -> none  [the longest x1 7.64 us: on_device(): lax.all_to_all(score_tiles, ('gr', 'gc'), split_axis=0, concat_axis=0, ti...]
    reshape x2 -> x0, local copies, waits for them, and re-layouts: 7.92 us -> none  [on_device(): means.reshape(CLUS_MEM, grid_rows, row_span, grid_cols, feature_span)]
    reduce_sum x2 -> x0, other arithmetic: 4.88 us -> none  [the longest x1 4.2 us: on_device(): slot_of = jnp.sum(onehot * cluster_slots[None, :], axis=1)]
  transfers between devices with their start and end apart: 4 -> 1, of which waited for: 2 -> 1; matrix products, arithmetic and copies ran while one was open for 22% -> 0% of each run, Pallas kernels for 0% -> 0%
where the time goes in v1:
time: 141 us
  blocking collectives  58.9 us (42%)
  Pallas kernels  37 us (26%)
  waiting for transfers between devices  36.9 us (26%)
  starting transfers between devices  4.26 us (3%)
  local copies, waits for them, and re-layouts  3.01 us (2%)
    all_to_all x1, blocking collectives, on_device(): lax.all_to_all(outgoing.reshape(16, 128, D), 'ingest', split_axis=0, conc...  46.2 us
    all_to_all x1, waiting for transfers between devices, on_device(): lax.all_to_all(tiles, ('gr', 'gc'), split_axis=0, concat_axis=0, tiled=True)  36.9 us
    pallas_call x1, Pallas kernels, cluster(): pl.pallas_call(functools.partial(ck, bq=bq), grid=(n,), in_specs=[pl.Bloc...  18.7 us
    pallas_call x1, Pallas kernels, gather(): pl.pallas_call(functools.partial(gk, NK=NK, PR=PR), in_specs=[pl.BlockSpe...  18.3 us
    all_to_all x1, blocking collectives, on_device(): lax.all_to_all(score_tiles, ('gr', 'gc'), split_axis=0, concat_axis=0, ti...  12.7 us
    all_to_all x1, starting transfers between devices, on_device(): lax.all_to_all(tiles, ('gr', 'gc'), split_axis=0, concat_axis=0, tiled=True)  4.26 us
    unnamed x3, local copies, waits for them, and re-layouts  2.97 us
  transfers between devices with their start and end apart: 1, of which 1 were waited for; matrix products, arithmetic and copies ran while one was open for 0% of the time, Pallas kernels for 0%

profile of v1, /device:TPU:1, one launch (start us, length us, event | category | flops | bytes accessed | tf_op | source)
XLA Modules:
  0.0 141.3 jit_solution(7759890680714468480)
XLA Ops:
  0.6 0.7 pad_add_fusion.par
  1.3 18.3 %shard_map.50 = bf16[2048,768]{1,0:T(8,128)(2,1)} custom-call(s32[2]{0:T(128)} %pad_add_fusion.par, s32[64,128]{1,0:T(8,128)} %bitcast.19, s32[1,128]{1,0:T(1,128)} %bitcast.22, bf16[8192,768]{1,0:T(8,128)(2,1)} %emb_ref.1), custom_call_target="tpu_custom_call" | custom-call | tf_op jit(solution)/shard_map/pallas_call | solution.py:108
  19.6 46.2 %all_to_all.15 = bf16[16,128,768]{2,1,0:T(8,128)(2,1)} all-to-all(bf16[16,128,768]{2,1,0:T(8,128)(2,1)} %bitcast.16), channel_id=1, replica_groups=mesh['ingest'=16,'gr'=4,'gc'=2] {'ingest'}, dimensions={0} | all-to-all | bytes 6291456 | tf_op jit(solution)/shard_map/all_to_all | solution.py:175
  65.8 18.7 %shard_map.51 = (bf16[4,2,512,384]{3,2,1,0:T(8,128)(2,1)}, f32[4,1,512]{2,1,0:T(1,128)}) custom-call(bf16[2048,768]{1,0:T(8,128)(2,1)} %bitcast.18), custom_call_target="tpu_custom_call" | custom-call | flops 12884901888 | bytes 6291456 | tf_op jit(solution)/shard_map/pallas_call | solution.py:151
  84.5 0.7 copy.11
  85.2 12.7 %all_to_all.16 = f32[8,1,512]{2,1,0:T(1,128)S(1)} all-to-all(f32[8,1,512]{2,1,0:T(1,128)S(1)} %broadcast_in_dim.11), channel_id=1, replica_groups=mesh['ingest'=16,'gr'=4,'gc'=2] {'gr','gc'}, dimensions={0} | all-to-all | bytes 32768 | tf_op jit(solution)/shard_map/all_to_all | solution.py:182
  97.9 4.3 %all-to-all-start.1 = ((bf16[8,1,512,384]{3,2,1,0:T(8,128)(2,1)}), bf16[8,1,512,384]{3,2,1,0:T(8,128)(2,1)S(1)}, u32[]{:S(2)}, u32[]{:S(2)}) async-start(bf16[8,1,512,384]{3,2,1,0:T(8,128)(2,1)} %bitcast.17), calls=%async_computation.1 | async-start | bytes 6291456 | tf_op jit(solution)/shard_map/all_to_all | solution.py:181
  102.1 0.6 copy.10
  102.8 36.9 %all-to-all-done.1 = bf16[8,1,512,384]{3,2,1,0:T(8,128)(2,1)S(1)} async-done(((bf16[8,1,512,384]{3,2,1,0:T(8,128)(2,1)}), bf16[8,1,512,384]{3,2,1,0:T(8,128)(2,1)S(1)}, u32[]{:S(2)}, u32[]{:S(2)}) %all-to-all-start.1) | async-done | bytes 3145760 | tf_op jit(solution)/shard_map/all_to_all | solution.py:181
  139.6 1.7 %copy.13 = bf16[8,512,384]{2,1,0:T(8,128)(2,1)} copy(bf16[8,512,384]{2,1,0:T(8,128)(2,1)S(1)} %bitcast.15) | data formatting | bytes 6291456
  (2 shorter events, 0.0 us)
Async XLA Ops:
  97.9 41.7 %all-to-all-start.1 = ((bf16[8,1,512,384]{3,2,1,0:T(8,128)(2,1)}), bf16[8,1,512,384]{3,2,1,0:T(8,128)(2,1)S(1)}, u32[]{:S(2)}, u32[]{:S(2)}) async-start(bf16[8,1,512,384]{3,2,1,0:T(8,128)(2,1)} %bitcast.17), calls=%async_computation.1 | async-start | bytes 6291456 | tf_op jit(solution)/shard_map/all_to_all | solution.py:181

commit v2 on v0

v2 whole, which is shorter than its diff:
```python
import jax
import jax.numpy as jnp
from jax import lax
from jax.experimental import pallas as pl
from jax.experimental.pallas import tpu as pltpu
from jax.sharding import PartitionSpec as P

D = 768
NT = (((1,), (1,)), ((), ()))
NN = (((1,), (0,)), ((), ()))
bf16 = jnp.bfloat16
f32 = jnp.float32


def dot(a, b, dn=NN):
    return lax.dot_general(a, b, dn, preferred_element_type=f32)


def iota(shape, d):
    return lax.broadcasted_iota(jnp.int32, shape, d)


ROWS = 8192
CH = ROWS // 128
NSEG = 8
NL = 4
GL = 16 // NL
W = 48
PR = 128
LCAP = GL * PR
CPAD = LCAP + 64


def gk(par, ids_ref, slots_ref, emb_ref, out_ref, C, emb_v, ev, rt, gref, rk, base_v, base_s, stage, sem, dsem, osem):
    seg = ROWS // NSEG
    cps = [
        pltpu.make_async_copy(
            emb_ref.at[pl.ds(s * seg, seg)], emb_v.at[pl.ds(s * seg, seg)], sem.at[s]
        )
        for s in range(NSEG)
    ]
    for c in cps:
        c.start()
    C[...] = jnp.zeros_like(C)
    want = iota((16, 128), 0) * 8 + par[0]
    cl = jnp.sum(jnp.where(slots_ref[...] == want, iota((16, 128), 1), 0), axis=1, keepdims=True)
    hot = (ids_ref[...][:, None, :] == cl[None, :, :]).astype(f32)
    hotb = hot.astype(bf16).reshape(CH * 16, 128)
    upper = (iota((128, 128), 0) < iota((128, 128), 1)).astype(bf16)
    ones = jnp.ones((128, 128), bf16)
    pre = dot(hotb, upper).reshape(CH, 16, 128)
    tot = dot(hotb, ones).reshape(CH, 16, 128)
    carry = jnp.ones((16, 128), f32)
    for a in range(CH):
        rk[a] = carry + pre[a]
        carry = carry + tot[a]
    own = (hot * rk[...]).astype(bf16).reshape(CH * 16, 128)
    r4 = iota((NL * CH, CH * 16), 0)
    c4 = iota((NL * CH, CH * 16), 1)
    pick = (((c4 >> 4) == (r4 & 63)) & (((c4 & 15) >> 2) == (r4 >> 6))).astype(bf16)
    rank4 = dot(pick, own)
    valid = rank4 > 0.0
    vb = valid.astype(f32).astype(bf16)
    rr = iota((NL * CH, NL * CH), 0)
    cc = iota((NL * CH, NL * CH), 1)
    lower = (((rr >> 6) == (cc >> 6)) & (cc < rr)).astype(bf16)
    tb = dot(vb, ones).astype(bf16)
    g = dot(lower, tb) + dot(vb, upper)
    gref[...] = jnp.where(valid, g, -1e6).astype(jnp.int32)
    trow = dot(jnp.ones((8, 128), bf16), vb, NT).astype(bf16)
    before = (iota((CH, 128), 0) < iota((CH, 128), 1)).astype(bf16)
    after = (iota((CH, 128), 0) < iota((CH, 128), 1) + 2).astype(bf16)
    lane = iota((8, 128), 1)
    chunk = (lane < CH) & ((lane & 1) == 0)
    over = jnp.zeros((8, 128), jnp.int32)
    for l in range(NL):
        counts = trow[:, l * CH : (l + 1) * CH]
        base = dot(counts, before).astype(jnp.int32)
        need = dot(counts, after).astype(jnp.int32) - (base & -16)
        over = jnp.maximum(over, jnp.where(chunk, need, 0))
        base_v[l * 8 : l * 8 + 8] = base
    cp = pltpu.make_async_copy(base_v, base_s, dsem)
    cp.start()
    rank = rank4[0:CH]
    val = jnp.where(valid[0:CH], g[0:CH] + 1.0, 0.0)
    for l in range(1, NL):
        s = slice(l * CH, (l + 1) * CH)
        rank = rank + rank4[s]
        val = val + jnp.where(valid[s], g[s] + 1.0, 0.0)
    hi = jnp.floor(val * (1.0 / 64.0))
    lo = val - 64.0 * hi
    pi = (iota((PR, 128), 0) + 1).astype(f32)
    for a in range(CH):
        s = slice(a * 128, (a + 1) * 128)
        rt[:, s] = (rank[a : a + 1] == pi).astype(bf16)
        ev[0:16, s] = (hot[a] * hi[a : a + 1]).astype(bf16)
        ev[16:32, s] = (hot[a] * lo[a : a + 1]).astype(bf16)
    hl = dot(rt[...], ev[...], NT)
    inv = 64.0 * hl[:, :16] + hl[:, 16:] - 1.0
    cp.wait()
    ji = iota((W, 256), 0)

    def window(i, l, w):
        al = base_s[l * 8, 2 * i] & -16
        return pl.multiple_of(al + w * W, 16)

    def grow(i, l):
        k = l * CH + 2 * i
        return jnp.concatenate([gref[pl.ds(k, 1), :], gref[pl.ds(k + 1, 1), :]], axis=1)

    UN = 4
    steps = seg // 256 // UN
    for s in range(NSEG):
        cps[s].wait()

        def body(j, _):
            for u in range(UN):
                i = j * UN + u
                x = emb_v[pl.ds(pl.multiple_of(i * 256, 256), 256), :]
                st = [window(i, l, 0) for l in range(NL)]
                p = jnp.concatenate(
                    [(grow(i, l) - st[l] == ji).astype(f32).astype(bf16) for l in range(NL)], axis=0
                )
                y = dot(p, x).astype(bf16)
                for l in range(NL):
                    C[l, pl.ds(st[l], W), :] = C[l, pl.ds(st[l], W), :] + y[l * W : (l + 1) * W]
            return 0

        lax.fori_loop(s * steps, (s + 1) * steps, body, 0)

    def rest(i, _):
        for l in range(NL):
            b0 = base_s[l * 8, 2 * i]
            need = base_s[l * 8, 2 * i + 2] - (b0 & -16)

            @pl.when(need > W)
            def _():
                x = emb_v[pl.ds(pl.multiple_of(i * 256, 256), 256), :]

                def win(w, _):
                    st = window(i, l, w)
                    y = dot((grow(i, l) - st == ji).astype(f32).astype(bf16), x).astype(bf16)
                    C[l, pl.ds(st, W), :] = C[l, pl.ds(st, W), :] + y
                    return 0

                lax.fori_loop(1, (need + W - 1) // W, win, 0)

        return 0

    @pl.when(jnp.max(over) > W)
    def _():
        lax.fori_loop(0, CH // 2, rest, 0)

    ki = iota((LCAP, LCAP), 1).astype(f32)
    first = iota((LCAP, 128), 1) == 0
    outs = []
    for l in range(NL):
        col = jnp.concatenate([inv[:, t : t + 1] for t in range(l * GL, (l + 1) * GL)], axis=0)
        y = dot((col == ki).astype(f32).astype(bf16), C[l, 0:LCAP, :])
        mark = y[:, 0:128] + jnp.where((col < 0.0) & first, 64.0, 0.0)
        stage[l, :, 0:128] = mark.astype(bf16)
        stage[l, :, 128:D] = y[:, 128:D].astype(bf16)
        cp = pltpu.make_async_copy(stage.at[l], out_ref.at[pl.ds(l * LCAP, LCAP)], osem.at[l])
        cp.start()
        outs.append(cp)
    for cp in outs:
        cp.wait()


def gather(par, ids, slots, emb):
    return pl.pallas_call(
        gk,
        in_specs=[
            pl.BlockSpec(memory_space=pltpu.SMEM),
            pl.BlockSpec(memory_space=pltpu.VMEM),
            pl.BlockSpec(memory_space=pltpu.VMEM),
            pl.BlockSpec(memory_space=pl.ANY),
        ],
        out_specs=pl.BlockSpec(memory_space=pltpu.HBM),
        out_shape=jax.ShapeDtypeStruct((16 * PR, D), bf16),
        scratch_shapes=[
            pltpu.VMEM((NL, CPAD, D), bf16),
            pltpu.VMEM((ROWS, D), bf16),
            pltpu.VMEM((32, ROWS), bf16),
            pltpu.VMEM((PR, ROWS), bf16),
            pltpu.VMEM((NL * CH, 128), jnp.int32),
            pltpu.VMEM((CH, 16, 128), f32),
            pltpu.VMEM((NL * 8, 128), jnp.int32),
            pltpu.SMEM((NL * 8, 128), jnp.int32),
            pltpu.VMEM((NL, LCAP, D), bf16),
            pltpu.SemaphoreType.DMA((NSEG,)),
            pltpu.SemaphoreType.DMA,
            pltpu.SemaphoreType.DMA((NL,)),
        ],
        compiler_params=pltpu.CompilerParams(vmem_limit_bytes=60 << 20),
    )(par, ids.reshape(CH, 128), slots.reshape(1, 128), emb)


CAP = 2048
BQ = 512
LOG2E = 1.4426950408889634
VM = pl.BlockSpec(memory_space=pltpu.VMEM)
SM = pl.BlockSpec(memory_space=pltpu.SMEM)
HB = pl.BlockSpec(memory_space=pltpu.HBM)
TILE = jax.ShapeDtypeStruct((BQ, 384), bf16)
SCORE = jax.ShapeDtypeStruct((1, BQ), f32)


def rows_of(k):
    return pl.ds(pl.multiple_of(k % 4 * BQ, BQ), BQ)


def finish(r, c, x_ref, tot, nb, keep_ref, swap_ref, sc_ref):
    un = x_ref[rows_of(r), 0:128][:, 0:1].astype(f32) > 32.0
    div = jnp.where(un, 1.0, tot)
    m = jnp.where(un, 0.0, nb / div).astype(bf16)
    lo, hi = m[:, :384], m[:, 384:]
    keep_ref[...] = jnp.where(c == 0, lo, hi)
    swap_ref[...] = jnp.where(c == 0, hi, lo)
    sc_ref[...] = jnp.broadcast_to(jnp.log(div), (BQ, 128)).T[0:1, :]


def query_block(r, c, x_ref, normed, bias, keep_ref, swap_ref, sc_ref):
    cos = dot(normed[rows_of(r), :], normed[...], NT)
    w = jnp.exp2(cos * (8.0 * LOG2E) + bias[0:1, :])
    tot = jnp.sum(w, axis=1, keepdims=True)
    nb = dot(w.astype(bf16), x_ref[...])
    finish(r, c, x_ref, tot, nb, keep_ref, swap_ref, sc_ref)


def query_block_fresh(r, c, x_ref, normed, bias, keep_ref, swap_ref, sc_ref):
    tot = jnp.zeros((BQ, 1), f32)
    nb = jnp.zeros((BQ, D), f32)
    e0 = (iota((8, D), 1) == 0).astype(bf16)
    for k in range(4):
        s = rows_of(r + k)
        x = x_ref[s, :]
        v = x.astype(f32)
        n = (v * lax.rsqrt(jnp.sum(v * v, axis=1, keepdims=True) + 1e-6)).astype(bf16)
        normed[s, :] = n
        b = jnp.where(dot(e0, x, NT) > 32.0, -1e30, -8.0 * LOG2E)
        bias[:, s] = b
        if k == 0:
            q = n
        w = jnp.exp2(dot(q, n, NT) * (8.0 * LOG2E) + b[0:1, :])
        tot = tot + jnp.sum(w, axis=1, keepdims=True)
        nb = nb + dot(w.astype(bf16), x)
    finish(r, c, x_ref, tot, nb, keep_ref, swap_ref, sc_ref)


def cost(blocks):
    return pl.CostEstimate(
        flops=4 * blocks * BQ * CAP * D,
        bytes_accessed=4 * CAP * D,
        transcendentals=blocks * BQ * CAP,
    )


def params():
    return pltpu.CompilerParams(vmem_limit_bytes=28 << 20)


def first_block(par, x):
    def kernel(p, x_ref, normed, bias, keep, swap, sc):
        query_block_fresh(p[1] + 2, p[2], x_ref, normed, bias, keep, swap, sc)

    return pl.pallas_call(
        kernel,
        in_specs=[SM, VM],
        out_specs=[VM] * 5,
        out_shape=[
            jax.ShapeDtypeStruct((CAP, D), bf16),
            jax.ShapeDtypeStruct((8, CAP), f32),
            TILE,
            TILE,
            SCORE,
        ],
        compiler_params=params(),
        cost_estimate=cost(1),
    )(par, x)


def next_blocks(par, x, normed, bias):
    def kernel(p, x_ref, normed, bias, k1, s1, c1, k3, s3, c3):
        query_block(p[1] + 1, p[2], x_ref, normed, bias, k1, s1, c1)
        query_block(p[1] + 3, p[2], x_ref, normed, bias, k3, s3, c3)

    return pl.pallas_call(
        kernel,
        in_specs=[SM, VM, VM, VM],
        out_specs=[VM] * 6,
        out_shape=[TILE, TILE, SCORE] * 2,
        compiler_params=params(),
        cost_estimate=cost(2),
    )(par, x, normed, bias)


def own_block(par, x, normed, bias, others):
    def kernel(p, x_ref, normed, bias, c1, c2, c3, out_ref, s0, scores, tile, c0, sem):
        query_block(p[1], p[2], x_ref, normed, bias, tile, s0, c0)
        cp = pltpu.make_async_copy(tile, out_ref.at[p[0]], sem)
        cp.start()
        for d, sc in enumerate((c0, c1, c2, c3)):
            for h in range(2):
                scores[(p[1] + d) % 4 * 2 + h] = sc[...]
        cp.wait()

    return pl.pallas_call(
        kernel,
        in_specs=[SM] + [VM] * 6,
        out_specs=[HB, VM, VM],
        out_shape=[
            jax.ShapeDtypeStruct((8, BQ, 384), bf16),
            TILE,
            jax.ShapeDtypeStruct((8, 1, BQ), f32),
        ],
        scratch_shapes=[
            pltpu.VMEM((BQ, 384), bf16),
            pltpu.VMEM((1, BQ), f32),
            pltpu.SemaphoreType.DMA,
        ],
        compiler_params=params(),
        cost_estimate=cost(1),
    )(par, x, normed, bias, *others)


def place(par, out, got):
    n = len(got)

    def kernel(p, *refs):
        out_ref, sem = refs[n + 1], refs[n + 2]
        cps = []
        for i, (dz, dc, _) in enumerate(got):
            at = (p[1] + 4 - dz) % 4 * 2 + (p[2] + dc) % 2
            cps.append(pltpu.make_async_copy(refs[i], out_ref.at[at], sem.at[i]))
            cps[-1].start()
        for cp in cps:
            cp.wait()

    return pl.pallas_call(
        kernel,
        in_specs=[SM] + [VM] * n + [HB],
        out_specs=HB,
        out_shape=jax.ShapeDtypeStruct(out.shape, out.dtype),
        input_output_aliases={n + 1: 0},
        scratch_shapes=[pltpu.SemaphoreType.DMA((n,))],
        compiler_params=pltpu.CompilerParams(vmem_limit_bytes=8 << 20),
    )(par, *[p for _, _, p in got], out)


def step(embeddings, cluster_ids, cluster_slots):
    z, c = lax.axis_index("gr"), lax.axis_index("gc")
    par = jnp.stack([z * 2 + c, z, c]).astype(jnp.int32)
    outgoing = gather(par, cluster_ids, cluster_slots, embeddings)
    arrived = lax.all_to_all(
        outgoing.reshape(16, PR, D), "ingest", split_axis=0, concat_axis=0, tiled=True
    )
    arrived, par = lax.optimization_barrier((arrived, par))
    x = arrived.reshape(CAP, D)

    def send(a, dz, dc):
        pairs = [(i, (i // 2 + dz) % 4 * 2 + (i % 2 + dc) % 2) for i in range(8)]
        return (dz, dc, lax.ppermute(a, ("gr", "gc"), pairs))

    normed, bias, k2, s2, c2 = first_block(par, x)
    got = [send(k2, 2, 0), send(s2, 2, 1)]
    k1, s1, c1, k3, s3, c3 = next_blocks(par, x, normed, bias)
    got += [send(k1, 1, 0), send(k3, 3, 0), send(s1, 1, 1), send(s3, 3, 1)]
    out, s0, scores = own_block(par, x, normed, bias, (c1, c2, c3))
    got += [send(s0, 0, 1)]
    dup_score = lax.all_to_all(scores, ("gr", "gc"), split_axis=0, concat_axis=0, tiled=True)
    out = place(par, out, got[:2])
    out = place(par, out, got[2:])
    return (out, dup_score.reshape(8, BQ))


def solution(mesh):
    return jax.shard_map(
        step,
        mesh=mesh,
        in_specs=(P("ingest", None), P("ingest", None), P()),
        out_specs=(P("ingest", "gr", "gc"), P("ingest", "gr")),
        check_vma=False,
    )
```

time: 221 us -> 107 us (0.48)
  waiting for transfers between devices: 81.8 us -> 0.02 us
  blocking collectives: 0 us -> 60.3 us
  local copies, waits for them, and re-layouts: 57.3 us -> 0.61 us
  matrix products: 39.2 us -> 0 us
  Pallas kernels: 0 us -> 32.1 us
  starting transfers between devices: 26.7 us -> 12.4 us
  other arithmetic: 14.6 us -> 0.65 us
    all_to_all x4 -> x0, waiting for transfers between devices: 81.8 us -> none  [the longest x1 45 us: on_device(): lax.all_to_all(outgoing, 'ingest', split_axis=1, concat_axis=1, tiled=True)]
    all_to_all x0 -> x2, blocking collectives: none -> 60.3 us  [the longest x1 46.1 us: step(): lax.all_to_all(outgoing.reshape(16, PR, D), 'ingest', split_axis=0, conca...]
    scatter x2 -> x0, local copies, waits for them, and re-layouts: 39.6 us -> none  [the longest x1 38.7 us: on_device(): jnp.zeros((total_slots, D), jnp.bfloat16).at[local_position]]
    dot_general x8 -> x0, matrix products: 39.2 us -> none  [the longest x4 22.1 us: one_block(): jnp.dot(normed_block, normed_all.T, preferred_element_type=jnp.float32)]
    pallas_call x0 -> x6, Pallas kernels: none -> 32.1 us  [the longest x1 10.5 us: gather(): pl.pallas_call(gk, in_specs=[pl.BlockSpec(memory_space=pltpu.SMEM), pl.Bl...]
    all_to_all x4 -> x0, starting transfers between devices: 26.7 us -> none  [the longest x1 7.64 us: on_device(): lax.all_to_all(score_tiles, ('gr', 'gc'), split_axis=0, concat_axis=0, ti...]
    ppermute x0 -> x7, starting transfers between devices: none -> 12.4 us  [send(): return (dz, dc, lax.ppermute(a, ('gr', 'gc'), pairs))]
    reshape x2 -> x0, local copies, waits for them, and re-layouts: 7.92 us -> none  [on_device(): means.reshape(CLUS_MEM, grid_rows, row_span, grid_cols, feature_span)]
  transfers between devices with their start and end apart: 4 -> 7, of which waited for: 2 -> 0; matrix products, arithmetic and copies ran while one was open for 22% -> 1% of each run, Pallas kernels for 0% -> 13%
where the time goes in v2:
time: 107 us
  blocking collectives  60.3 us (56%)
  Pallas kernels  32.1 us (30%)
  starting transfers between devices  12.4 us (12%)
    all_to_all x1, blocking collectives, step(): lax.all_to_all(outgoing.reshape(16, PR, D), 'ingest', split_axis=0, conca...  46.1 us
    all_to_all x1, blocking collectives, step(): lax.all_to_all(scores, ('gr', 'gc'), split_axis=0, concat_axis=0, tiled=T...  14.2 us
    ppermute x7, starting transfers between devices, send(): return (dz, dc, lax.ppermute(a, ('gr', 'gc'), pairs))  12.4 us
    pallas_call x1, Pallas kernels, gather(): pl.pallas_call(gk, in_specs=[pl.BlockSpec(memory_space=pltpu.SMEM), pl.Bl...  10.5 us
    pallas_call x1, Pallas kernels, next_blocks(): pl.pallas_call(kernel, in_specs=[SM, VM, VM, VM], out_specs=[VM] * 6, out...  7.66 us
    pallas_call x1, Pallas kernels, first_block(): pl.pallas_call(kernel, in_specs=[SM, VM], out_specs=[VM] * 5, out_shape=[...  5.58 us
    pallas_call x1, Pallas kernels, own_block(): pl.pallas_call(kernel, in_specs=[SM] + [VM] * 6, out_specs=[HB, VM, VM],...  4.97 us
    pallas_call x2, Pallas kernels, place(): pl.pallas_call(kernel, in_specs=[SM] + [VM] * n + [HB], out_specs=HB, out...  3.3 us
  transfers between devices with their start and end apart: 7, of which 0 were waited for; matrix products, arithmetic and copies ran while one was open for 1% of the time, Pallas kernels for 13%

profile of v2, /device:TPU:1, one launch (start us, length us, event | category | flops | bytes accessed | tf_op | source)
XLA Modules:
  0.0 106.9 jit_solution(2345095346128101744)
XLA Ops:
  0.6 0.7 pad_add_fusion.par.p
  1.3 10.5 %shard_map.50 = bf16[2048,768]{1,0:T(8,128)(2,1)} custom-call(s32[3]{0:T(128)} %pad_add_fusion.par.p, s32[64,128]{1,0:T(8,128)} %bitcast.14, s32[1,128]{1,0:T(1,128)} %bitcast.16, bf16[8192,768]{1,0:T(8,128)(2,1)} %emb_ref.1), custom_call_target="tpu_custom_call" | custom-call | tf_op jit(solution)/shard_map/pallas_call | solution.py:171
  11.8 46.1 %all_to_all.10 = bf16[16,128,768]{2,1,0:T(8,128)(2,1)S(1)} all-to-all(bf16[16,128,768]{2,1,0:T(8,128)(2,1)} %bitcast.13), channel_id=1, replica_groups=mesh['ingest'=16,'gr'=4,'gc'=2] {'ingest'}, dimensions={0} | all-to-all | bytes 6291456 | tf_op jit(solution)/shard_map/all_to_all | solution.py:355
  57.9 5.6 %shard_map.51 = (bf16[2048,768]{1,0:T(8,128)(2,1)S(1)}, f32[8,2048]{1,0:T(8,128)S(1)}, bf16[512,384]{1,0:T(8,128)(2,1)S(1)}, bf16[512,384]{1,0:T(8,128)(2,1)S(1)}, f32[1,512]{1,0:T(1,128)S(1)}) custom-call(s32[3]{0:T(128)S(1)} %copy-done, bf16[2048,768]{1,0:T(8,128)(2,1)S(1)} %bitcast.10), custom_call_target="tpu_custom_call" | custom-call | flops 3221225472 | bytes 6291456 | tf_op jit(solution)/shard_map/pallas_call | solution.py:267
  63.5 3.7 %collective-permute-start.5 = (bf16[512,384]{1,0:T(8,128)(2,1)S(1)}, bf16[512,384]{1,0:T(8,128)(2,1)S(1)}, u32[]{:S(2)}, u32[]{:S(2)}) collective-permute-start(bf16[512,384]{1,0:T(8,128)(2,1)S(1)} %get-tuple-element.30), channel_id=1, source_target_pairs={{0,4},{1,5},{2,6},{3,7},{4,0},{5,1},{6,2},{7,3},{8,12},{9,13},{10,... | collective-permute-start | bytes 1179656 | tf_op jit(solution)/shard_map/ppermute | solution.py:363
  67.2 2.0 %collective-permute-start.6 = (bf16[512,384]{1,0:T(8,128)(2,1)S(1)}, bf16[512,384]{1,0:T(8,128)(2,1)S(1)}, u32[]{:S(2)}, u32[]{:S(2)}) collective-permute-start(bf16[512,384]{1,0:T(8,128)(2,1)S(1)} %get-tuple-element.31), channel_id=1, source_target_pairs={{0,5},{1,4},{2,7},{3,6},{4,1},{5,0},{6,3},{7,2},{8,13},{9,12},{10,... | collective-permute-start | bytes 1179656 | tf_op jit(solution)/shard_map/ppermute | solution.py:363
  69.2 7.7 %shard_map.52 = (bf16[512,384]{1,0:T(8,128)(2,1)S(1)}, bf16[512,384]{1,0:T(8,128)(2,1)S(1)}, f32[1,512]{1,0:T(1,128)S(1)}, bf16[512,384]{1,0:T(8,128)(2,1)S(1)},...) custom-call(s32[3]{0:T(128)S(1)} %copy-done, bf16[2048,768]{1,0:T(8,128)(2,1)S(1)} %bitcast.11, ...), custom_call_target="tpu_custom_call" | custom-call | flops 6442450944 | bytes 6291456 | tf_op jit(solution)/shard_map/pallas_call | solution.py:288
  76.9 1.3 %collective-permute-start = (bf16[512,384]{1,0:T(8,128)(2,1)S(1)}, bf16[512,384]{1,0:T(8,128)(2,1)S(1)}, u32[]{:S(2)}, u32[]{:S(2)}) collective-permute-start(bf16[512,384]{1,0:T(8,128)(2,1)S(1)} %get-tuple-element.22), channel_id=1, source_target_pairs={{0,2},{1,3},{2,4},{3,5},{4,6},{5,7},{6,0},{7,1},{8,10},{9,11},{10,... | collective-permute-start | bytes 1179656 | tf_op jit(solution)/shard_map/ppermute | solution.py:363
  78.2 2.2 %collective-permute-start.1 = (bf16[512,384]{1,0:T(8,128)(2,1)S(1)}, bf16[512,384]{1,0:T(8,128)(2,1)S(1)}, u32[]{:S(2)}, u32[]{:S(2)}) collective-permute-start(bf16[512,384]{1,0:T(8,128)(2,1)S(1)} %get-tuple-element.23), channel_id=1, source_target_pairs={{0,6},{1,7},{2,0},{3,1},{4,2},{5,3},{6,4},{7,5},{8,14},{9,15},{10,... | collective-permute-start | bytes 1179656 | tf_op jit(solution)/shard_map/ppermute | solution.py:363
  80.4 0.0 collective-permute-start.2
  80.4 5.0 %shard_map.53 = (bf16[8,512,384]{2,1,0:T(8,128)(2,1)}, bf16[512,384]{1,0:T(8,128)(2,1)S(1)}, f32[8,1,512]{2,1,0:T(1,128)S(1)}) custom-call(s32[3]{0:T(128)S(1)} %copy-done, bf16[2048,768]{1,0:T(8,128)(2,1)S(1)} %bitcast.12, bf16[2048,768]{1,0:T(8,128)(2,1)S(1)} %get-tuple-element.20.normed, f32[8,2048]{1,0:T(8,128)S(1)} %get-tuple-element.21.bias, ...), custom_call_target="tpu_custom_call" | custom-call | flops 3221225472 | bytes 6291456 | tf_op jit(solution)/shard_map/pallas_call | solution.py:308
  85.4 0.0 collective-permute-done.5.refs_0_
  85.4 3.0 %collective-permute-start.3 = (bf16[512,384]{1,0:T(8,128)(2,1)S(1)}, bf16[512,384]{1,0:T(8,128)(2,1)S(1)}, u32[]{:S(2)}, u32[]{:S(2)}) collective-permute-start(bf16[512,384]{1,0:T(8,128)(2,1)S(1)} %get-tuple-element.25), channel_id=1, source_target_pairs={{0,7},{1,6},{2,1},{3,0},{4,3},{5,2},{6,5},{7,4},{8,15},{9,14},{10,... | collective-permute-start | bytes 1179656 | tf_op jit(solution)/shard_map/ppermute | solution.py:363
  88.4 0.0 collective-permute-done.6.refs_1_
  88.4 0.1 collective-permute-start.4
  88.5 14.2 %all_to_all.11 = f32[8,1,512]{2,1,0:T(1,128)S(1)} all-to-all(f32[8,1,512]{2,1,0:T(1,128)S(1)} %get-tuple-element.33), channel_id=1, replica_groups=mesh['ingest'=16,'gr'=4,'gc'=2] {'gr','gc'}, dimensions={0} | all-to-all | bytes 32768 | tf_op jit(solution)/shard_map/all_to_all | solution.py:371
  102.7 0.6 copy.9
  103.3 1.4 %shard_map.54.refs_5_ = bf16[8,512,384]{2,1,0:T(8,128)(2,1)} custom-call(s32[3]{0:T(128)S(1)} %copy-done, bf16[512,384]{1,0:T(8,128)(2,1)S(1)} %collective-permute-done.5.refs_0_, bf16[512,384]{1,0:T(8,128)(2,1)S(1)} %collective-permute-done.6.refs_1_, bf16[8,512,384]{2,1,0:T(8,128)(2,1)} %get-tuple-element.32.refs_2_), custom_call_target="tpu_custom_call", output_to_operand_aliasing={{}: (3, {})} | custom-call | tf_op jit(solution)/shard_map/pallas_call | solution.py:340
  104.8 0.0 collective-permute-done.refs_0_
  104.8 0.0 collective-permute-done.1.refs_1_
  104.8 0.0 collective-permute-done.2.refs_2_
  104.8 0.0 collective-permute-done.3.refs_3_
  104.8 0.0 collective-permute-done.4.refs_4_
  104.8 1.9 %shard_map.55 = bf16[8,512,384]{2,1,0:T(8,128)(2,1)} custom-call(s32[3]{0:T(128)S(1)} %copy-done, bf16[512,384]{1,0:T(8,128)(2,1)S(1)} %collective-permute-done.refs_0_, bf16[512,384]{1,0:T(8,128)(2,1)S(1)} %collective-permute-done.1.refs_1_, bf16[512,384]{1,0:T(8,128)(2,1)S(1)} %collective-permute-done.2.refs_2_, ...), custom_call_target="tpu_custom_call", output_to_operand_aliasing={{}: (6, {})} | custom-call | tf_op jit(solution)/shard_map/pallas_call | solution.py:340
  (2 shorter events, 0.0 us)
Async XLA Ops:
  11.8 46.1 %copy-start = (s32[3]{0:T(128)S(1)}, s32[3]{0:T(128)}, u32[]{:S(2)}) copy-start(s32[3]{0:T(128)} %pad_add_fusion.par.p) | copy-start | bytes 40
  63.5 21.9 %collective-permute-start.5 = (bf16[512,384]{1,0:T(8,128)(2,1)S(1)}, bf16[512,384]{1,0:T(8,128)(2,1)S(1)}, u32[]{:S(2)}, u32[]{:S(2)}) collective-permute-start(bf16[512,384]{1,0:T(8,128)(2,1)S(1)} %get-tuple-element.30), channel_id=1, source_target_pairs={{0,4},{1,5},{2,6},{3,7},{4,0},{5,1},{6,2},{7,3},{8,12},{9,13},{10,... | collective-permute-start | bytes 1179656 | tf_op jit(solution)/shard_map/ppermute | solution.py:363
  67.2 21.2 %collective-permute-start.6 = (bf16[512,384]{1,0:T(8,128)(2,1)S(1)}, bf16[512,384]{1,0:T(8,128)(2,1)S(1)}, u32[]{:S(2)}, u32[]{:S(2)}) collective-permute-start(bf16[512,384]{1,0:T(8,128)(2,1)S(1)} %get-tuple-element.31), channel_id=1, source_target_pairs={{0,5},{1,4},{2,7},{3,6},{4,1},{5,0},{6,3},{7,2},{8,13},{9,12},{10,... | collective-permute-start | bytes 1179656 | tf_op jit(solution)/shard_map/ppermute | solution.py:363
  76.9 27.9 %collective-permute-start = (bf16[512,384]{1,0:T(8,128)(2,1)S(1)}, bf16[512,384]{1,0:T(8,128)(2,1)S(1)}, u32[]{:S(2)}, u32[]{:S(2)}) collective-permute-start(bf16[512,384]{1,0:T(8,128)(2,1)S(1)} %get-tuple-element.22), channel_id=1, source_target_pairs={{0,2},{1,3},{2,4},{3,5},{4,6},{5,7},{6,0},{7,1},{8,10},{9,11},{10,... | collective-permute-start | bytes 1179656 | tf_op jit(solution)/shard_map/ppermute | solution.py:363
  78.2 26.6 %collective-permute-start.1 = (bf16[512,384]{1,0:T(8,128)(2,1)S(1)}, bf16[512,384]{1,0:T(8,128)(2,1)S(1)}, u32[]{:S(2)}, u32[]{:S(2)}) collective-permute-start(bf16[512,384]{1,0:T(8,128)(2,1)S(1)} %get-tuple-element.23), channel_id=1, source_target_pairs={{0,6},{1,7},{2,0},{3,1},{4,2},{5,3},{6,4},{7,5},{8,14},{9,15},{10,... | collective-permute-start | bytes 1179656 | tf_op jit(solution)/shard_map/ppermute | solution.py:363
  80.4 24.4 %collective-permute-start.2 = (bf16[512,384]{1,0:T(8,128)(2,1)S(1)}, bf16[512,384]{1,0:T(8,128)(2,1)S(1)}, u32[]{:S(2)}, u32[]{:S(2)}) collective-permute-start(bf16[512,384]{1,0:T(8,128)(2,1)S(1)} %get-tuple-element.24), channel_id=1, source_target_pairs={{0,3},{1,2},{2,5},{3,4},{4,7},{5,6},{6,1},{7,0},{8,11},{9,10},{10,... | collective-permute-start | bytes 1179656 | tf_op jit(solution)/shard_map/ppermute | solution.py:363
  85.4 19.4 %collective-permute-start.3 = (bf16[512,384]{1,0:T(8,128)(2,1)S(1)}, bf16[512,384]{1,0:T(8,128)(2,1)S(1)}, u32[]{:S(2)}, u32[]{:S(2)}) collective-permute-start(bf16[512,384]{1,0:T(8,128)(2,1)S(1)} %get-tuple-element.25), channel_id=1, source_target_pairs={{0,7},{1,6},{2,1},{3,0},{4,3},{5,2},{6,5},{7,4},{8,15},{9,14},{10,... | collective-permute-start | bytes 1179656 | tf_op jit(solution)/shard_map/ppermute | solution.py:363
  88.4 16.4 %collective-permute-start.4 = (bf16[512,384]{1,0:T(8,128)(2,1)S(1)}, bf16[512,384]{1,0:T(8,128)(2,1)S(1)}, u32[]{:S(2)}, u32[]{:S(2)}) collective-permute-start(bf16[512,384]{1,0:T(8,128)(2,1)S(1)} %get-tuple-element.29), channel_id=1, source_target_pairs={{0,1},{1,0},{2,3},{3,2},{4,5},{5,4},{6,7},{7,6},{8,9},{9,8},{10,11... | collective-permute-start | bytes 1179656 | tf_op jit(solution)/shard_map/ppermute | solution.py:363

commit v3 on v2

--- a/solution.py
+++ b/solution.py
@@ -31,7 +31,7 @@
 CPAD = LCAP + 64
 
 
-def gk(par, ids_ref, slots_ref, emb_ref, out_ref, C, emb_v, ev, rt, gref, rk, base_v, base_s, stage, sem, dsem, osem):
+def gk(ids_ref, slots_ref, emb_ref, out_ref, C, emb_v, ev, rt, gref, rk, base_v, base_s, stage, sem, dsem, osem):
     seg = ROWS // NSEG
     cps = [
         pltpu.make_async_copy(
@@ -42,7 +42,7 @@
     for c in cps:
         c.start()
     C[...] = jnp.zeros_like(C)
-    want = iota((16, 128), 0) * 8 + par[0]
+    want = iota((16, 128), 0) * 8 + lax.axis_index("gr") * 2 + lax.axis_index("gc")
     cl = jnp.sum(jnp.where(slots_ref[...] == want, iota((16, 128), 1), 0), axis=1, keepdims=True)
     hot = (ids_ref[...][:, None, :] == cl[None, :, :]).astype(f32)
     hotb = hot.astype(bf16).reshape(CH * 16, 128)
@@ -167,11 +167,10 @@
         cp.wait()
 
 
-def gather(par, ids, slots, emb):
+def gather(ids, slots, emb):
     return pl.pallas_call(
         gk,
         in_specs=[
-            pl.BlockSpec(memory_space=pltpu.SMEM),
             pl.BlockSpec(memory_space=pltpu.VMEM),
             pl.BlockSpec(memory_space=pltpu.VMEM),
             pl.BlockSpec(memory_space=pl.ANY),
@@ -193,7 +192,7 @@
             pltpu.SemaphoreType.DMA((NL,)),
         ],
         compiler_params=pltpu.CompilerParams(vmem_limit_bytes=60 << 20),
-    )(par, ids.reshape(CH, 128), slots.reshape(1, 128), emb)
+    )(ids.reshape(CH, 128), slots.reshape(1, 128), emb)
 
 
 CAP = 2048
@@ -202,116 +201,106 @@
 VM = pl.BlockSpec(memory_space=pltpu.VMEM)
 SM = pl.BlockSpec(memory_space=pltpu.SMEM)
 HB = pl.BlockSpec(memory_space=pltpu.HBM)
-TILE = jax.ShapeDtypeStruct((BQ, 384), bf16)
-SCORE = jax.ShapeDtypeStruct((1, BQ), f32)
-
-
-def rows_of(k):
-    return pl.ds(pl.multiple_of(k % 4 * BQ, BQ), BQ)
-
-
-def finish(r, c, x_ref, tot, nb, keep_ref, swap_ref, sc_ref):
-    un = x_ref[rows_of(r), 0:128][:, 0:1].astype(f32) > 32.0
+
+
+def rows_of(block, start=0, count=BQ):
+    return pl.ds(pl.multiple_of(block % 4 * BQ + start, 128), count)
+
+
+def position():
+    return lax.axis_index("gr"), lax.axis_index("gc")
+
+
+def query_rows(rows, x_ref, normed, bias, keep_ref, swap_ref, sc_ref):
+    cos = dot(normed[rows, :], normed[...], NT)
+    w = jnp.exp2(cos * (8.0 * LOG2E) + bias[0:1, :])
+    tot = jnp.sum(w, axis=1, keepdims=True)
+    nb = dot(w.astype(bf16), x_ref[...])
+    un = x_ref[rows, 0:128][:, 0:1].astype(f32) > 32.0
     div = jnp.where(un, 1.0, tot)
     m = jnp.where(un, 0.0, nb / div).astype(bf16)
     lo, hi = m[:, :384], m[:, 384:]
-    keep_ref[...] = jnp.where(c == 0, lo, hi)
-    swap_ref[...] = jnp.where(c == 0, hi, lo)
-    sc_ref[...] = jnp.broadcast_to(jnp.log(div), (BQ, 128)).T[0:1, :]
-
-
-def query_block(r, c, x_ref, normed, bias, keep_ref, swap_ref, sc_ref):
-    cos = dot(normed[rows_of(r), :], normed[...], NT)
-    w = jnp.exp2(cos * (8.0 * LOG2E) + bias[0:1, :])
-    tot = jnp.sum(w, axis=1, keepdims=True)
-    nb = dot(w.astype(bf16), x_ref[...])
-    finish(r, c, x_ref, tot, nb, keep_ref, swap_ref, sc_ref)
-
-
-def query_block_fresh(r, c, x_ref, normed, bias, keep_ref, swap_ref, sc_ref):
-    tot = jnp.zeros((BQ, 1), f32)
-    nb = jnp.zeros((BQ, D), f32)
-    e0 = (iota((8, D), 1) == 0).astype(bf16)
-    for k in range(4):
-        s = rows_of(r + k)
-        x = x_ref[s, :]
-        v = x.astype(f32)
-        n = (v * lax.rsqrt(jnp.sum(v * v, axis=1, keepdims=True) + 1e-6)).astype(bf16)
-        normed[s, :] = n
-        b = jnp.where(dot(e0, x, NT) > 32.0, -1e30, -8.0 * LOG2E)
-        bias[:, s] = b
-        if k == 0:
-            q = n
-        w = jnp.exp2(dot(q, n, NT) * (8.0 * LOG2E) + b[0:1, :])
-        tot = tot + jnp.sum(w, axis=1, keepdims=True)
-        nb = nb + dot(w.astype(bf16), x)
-    finish(r, c, x_ref, tot, nb, keep_ref, swap_ref, sc_ref)
-
-
-def cost(blocks):
+    even = lax.axis_index("gc") == 0
+    keep_ref[...] = jnp.where(even, lo, hi)
+    swap_ref[...] = jnp.where(even, hi, lo)
+    sc_ref[...] = jnp.broadcast_to(jnp.log(div), (rows.size, 128)).T[0:1, :]
+
+
+def cost(rows):
     return pl.CostEstimate(
-        flops=4 * blocks * BQ * CAP * D,
-        bytes_accessed=4 * CAP * D,
-        transcendentals=blocks * BQ * CAP,
+        flops=4 * rows * CAP * D, bytes_accessed=4 * CAP * D, transcendentals=rows * CAP
     )
 
 
-def params():
-    return pltpu.CompilerParams(vmem_limit_bytes=28 << 20)
-
-
-def first_block(par, x):
-    def kernel(p, x_ref, normed, bias, keep, swap, sc):
-        query_block_fresh(p[1] + 2, p[2], x_ref, normed, bias, keep, swap, sc)
+def params(mib=28):
+    return pltpu.CompilerParams(vmem_limit_bytes=mib << 20)
+
+
+def tiles(rows):
+    t = jax.ShapeDtypeStruct((rows, 384), bf16)
+    return [t, t, jax.ShapeDtypeStruct((1, rows), f32)]
+
+
+def first_rows(x):
+    def kernel(x_ref, normed, bias, *outs):
+        for k in range(CAP // 256):
+            s = pl.ds(k * 256, 256)
+            v = x_ref[s, :].astype(f32)
+            sq = jnp.sum(v * v, axis=1, keepdims=True)
+            normed[s, :] = (v * lax.rsqrt(sq + 1e-6)).astype(bf16)
+        e0 = (iota((8, D), 1) == 0).astype(bf16)
+        bias[...] = jnp.where(dot(e0, x_ref[...], NT) > 32.0, -1e30, -8.0 * LOG2E)
+        query_rows(rows_of(position()[0] + 2, 0, 512), x_ref, normed, bias, *outs)
 
     return pl.pallas_call(
         kernel,
-        in_specs=[SM, VM],
+        in_specs=[VM],
         out_specs=[VM] * 5,
         out_shape=[
             jax.ShapeDtypeStruct((CAP, D), bf16),
             jax.ShapeDtypeStruct((8, CAP), f32),
-            TILE,
-            TILE,
-            SCORE,
+            *tiles(512),
         ],
         compiler_params=params(),
-        cost_estimate=cost(1),
-    )(par, x)
-
-
-def next_blocks(par, x, normed, bias):
-    def kernel(p, x_ref, normed, bias, k1, s1, c1, k3, s3, c3):
-        query_block(p[1] + 1, p[2], x_ref, normed, bias, k1, s1, c1)
-        query_block(p[1] + 3, p[2], x_ref, normed, bias, k3, s3, c3)
-
+        cost_estimate=cost(512),
+    )(x)
+
+
+def more_rows(x, normed, bias, spans):
+    def kernel(x_ref, normed, bias, *outs):
+        for i, (d, start, count) in enumerate(spans):
+            rows = rows_of(position()[0] + d, start, count)
+            query_rows(rows, x_ref, normed, bias, *outs[3 * i : 3 * i + 3])
+
+    n = len(spans)
     return pl.pallas_call(
         kernel,
-        in_specs=[SM, VM, VM, VM],
-        out_specs=[VM] * 6,
-        out_shape=[TILE, TILE, SCORE] * 2,
+        in_specs=[VM, VM, VM],
+        out_specs=[VM] * (3 * n),
+        out_shape=[t for _, _, count in spans for t in tiles(count)],
         compiler_params=params(),
-        cost_estimate=cost(2),
-    )(par, x, normed, bias)
-
-
-def own_block(par, x, normed, bias, others):
-    def kernel(p, x_ref, normed, bias, c1, c2, c3, out_ref, s0, scores, tile, c0, sem):
-        query_block(p[1], p[2], x_ref, normed, bias, tile, s0, c0)
-        cp = pltpu.make_async_copy(tile, out_ref.at[p[0]], sem)
+        cost_estimate=cost(sum(count for _, _, count in spans)),
+    )(x, normed, bias)
+
+
+def own_block(x, normed, bias, others):
+    def kernel(x_ref, normed, bias, c1, c2, c3, out_ref, s0, scores, tile, c0, sem):
+        z, c = position()
+        query_rows(rows_of(z), x_ref, normed, bias, tile, s0, c0)
+        cp = pltpu.make_async_copy(tile, out_ref.at[z * 2 + c], sem)
         cp.start()
-        for d, sc in enumerate((c0, c1, c2, c3)):
+        for d, sc in enumerate((c0[...], c1[...], c2[...], c3[...])):
             for h in range(2):
-                scores[(p[1] + d) % 4 * 2 + h] = sc[...]
+                scores[(z + d) % 4 * 2 + h] = sc
         cp.wait()
 
     return pl.pallas_call(
         kernel,
-        in_specs=[SM] + [VM] * 6,
+        in_specs=[VM] * 6,
         out_specs=[HB, VM, VM],
         out_shape=[
             jax.ShapeDtypeStruct((8, BQ, 384), bf16),
-            TILE,
+            jax.ShapeDtypeStruct((BQ, 384), bf16),
             jax.ShapeDtypeStruct((8, 1, BQ), f32),
         ],
         scratch_shapes=[
@@ -320,58 +309,61 @@
             pltpu.SemaphoreType.DMA,
         ],
         compiler_params=params(),
-        cost_estimate=cost(1),
-    )(par, x, normed, bias, *others)
-
-
-def place(par, out, got):
+        cost_estimate=cost(BQ),
+    )(x, normed, bias, *others)
+
+
+def place(out, got, scores=None):
     n = len(got)
-
-    def kernel(p, *refs):
-        out_ref, sem = refs[n + 1], refs[n + 2]
+    k = 0 if scores is None else 1
+
+    def kernel(*refs):
+        z, c = position()
+        out_ref, sem = refs[n + 1 + k], refs[-1]
         cps = []
-        for i, (dz, dc, _) in enumerate(got):
-            at = (p[1] + 4 - dz) % 4 * 2 + (p[2] + dc) % 2
-            cps.append(pltpu.make_async_copy(refs[i], out_ref.at[at], sem.at[i]))
+        for i, (dz, dc, start, piece) in enumerate(got):
+            at = (z + 4 - dz) % 4 * 2 + (c + dc) % 2
+            target = out_ref.at[at, pl.ds(start, piece.shape[0])]
+            cps.append(pltpu.make_async_copy(refs[i], target, sem.at[i]))
             cps[-1].start()
+        if k:
+            for q in range(8):
+                refs[n + 2 + k][q : q + 1, :] = refs[n + 1][q]
         for cp in cps:
             cp.wait()
 
+    results = [jax.ShapeDtypeStruct(out.shape, out.dtype), jax.ShapeDtypeStruct((8, BQ), f32)]
     return pl.pallas_call(
         kernel,
-        in_specs=[SM] + [VM] * n + [HB],
-        out_specs=HB,
-        out_shape=jax.ShapeDtypeStruct(out.shape, out.dtype),
-        input_output_aliases={n + 1: 0},
+        in_specs=[VM] * n + [HB] + [VM] * k,
+        out_specs=[HB, VM][: 1 + k],
+        out_shape=results[: 1 + k],
+        input_output_aliases={n: 0},
         scratch_shapes=[pltpu.SemaphoreType.DMA((n,))],
-        compiler_params=pltpu.CompilerParams(vmem_limit_bytes=8 << 20),
-    )(par, *[p for _, _, p in got], out)
+        compiler_params=params(8),
+    )(*[p for _, _, _, p in got], out, *([scores] if k else []))
 
 
 def step(embeddings, cluster_ids, cluster_slots):
-    z, c = lax.axis_index("gr"), lax.axis_index("gc")
-    par = jnp.stack([z * 2 + c, z, c]).astype(jnp.int32)
-    outgoing = gather(par, cluster_ids, cluster_slots, embeddings)
+    outgoing = gather(cluster_ids, cluster_slots, embeddings)
     arrived = lax.all_to_all(
         outgoing.reshape(16, PR, D), "ingest", split_axis=0, concat_axis=0, tiled=True
     )
-    arrived, par = lax.optimization_barrier((arrived, par))
     x = arrived.reshape(CAP, D)
 
-    def send(a, dz, dc):
+    def send(a, dz, dc, start=0):
         pairs = [(i, (i // 2 + dz) % 4 * 2 + (i % 2 + dc) % 2) for i in range(8)]
-        return (dz, dc, lax.ppermute(a, ("gr", "gc"), pairs))
-
-    normed, bias, k2, s2, c2 = first_block(par, x)
+        return (dz, dc, start, lax.ppermute(a, ("gr", "gc"), pairs))
+
+    normed, bias, k2, s2, c2 = first_rows(x)
     got = [send(k2, 2, 0), send(s2, 2, 1)]
-    k1, s1, c1, k3, s3, c3 = next_blocks(par, x, normed, bias)
-    got += [send(k1, 1, 0), send(k3, 3, 0), send(s1, 1, 1), send(s3, 3, 1)]
-    out, s0, scores = own_block(par, x, normed, bias, (c1, c2, c3))
+    k1, s1, c1, k3, s3, c3 = more_rows(x, normed, bias, [(1, 0, BQ), (3, 0, BQ)])
+    last = [send(s1, 1, 1), send(s3, 3, 1), send(k1, 1, 0), send(k3, 3, 0)]
+    out, s0, scores = own_block(x, normed, bias, (c1, c2, c3))
     got += [send(s0, 0, 1)]
-    dup_score = lax.all_to_all(scores, ("gr", "gc"), split_axis=0, concat_axis=0, tiled=True)
-    out = place(par, out, got[:2])
-    out = place(par, out, got[2:])
-    return (out, dup_score.reshape(8, BQ))
+    scores = lax.all_to_all(scores, ("gr", "gc"), split_axis=0, concat_axis=0, tiled=True)
+    (out,) = place(out, got)
+    return tuple(place(out, last, scores))
 
 
 def solution(mesh):

time: 107 us -> 105 us (0.981)
  blocking collectives: 60.3 us -> 46.1 us
  waiting for transfers between devices: 0.02 us -> 11.4 us
  starting transfers between devices: 12.4 us -> 15 us
    all_to_all x1 -> x0, blocking collectives: 14.2 us -> none  [step(): lax.all_to_all(scores, ('gr', 'gc'), split_axis=0, concat_axis=0, tiled=T...]
    all_to_all x0 -> x1, waiting for transfers between devices: none -> 10.3 us  [step(): lax.all_to_all(scores, ('gr', 'gc'), split_axis=0, concat_axis=0, tiled=T...]
    all_to_all x0 -> x1, starting transfers between devices: none -> 3.88 us  [step(): lax.all_to_all(scores, ('gr', 'gc'), split_axis=0, concat_axis=0, tiled=T...]
    ppermute x7, starting transfers between devices: 12.4 us -> 11.1 us  [send(): return (dz, dc, start, lax.ppermute(a, ('gr', 'gc'), pairs))]
    ppermute x7, waiting for transfers between devices: 0.02 us -> 1.14 us  [send(): return (dz, dc, start, lax.ppermute(a, ('gr', 'gc'), pairs))]
  transfers between devices with their start and end apart: 7 -> 8, of which waited for: 0 -> 2; matrix products, arithmetic and copies ran while one was open for 1% -> 0% of each run, Pallas kernels for 13% -> 13%
where the time goes in v3:
time: 105 us
  blocking collectives  46.1 us (44%)
  Pallas kernels  31.7 us (30%)
  starting transfers between devices  15 us (14%)
  waiting for transfers between devices  11.4 us (11%)
    all_to_all x1, blocking collectives, step(): lax.all_to_all(outgoing.reshape(16, PR, D), 'ingest', split_axis=0, conca...  46.1 us
    ppermute x7, starting transfers between devices, send(): return (dz, dc, start, lax.ppermute(a, ('gr', 'gc'), pairs))  11.1 us
    pallas_call x1, Pallas kernels, gather(): pl.pallas_call(gk, in_specs=[pl.BlockSpec(memory_space=pltpu.VMEM), pl.Bl...  10.6 us
    all_to_all x1, waiting for transfers between devices, step(): lax.all_to_all(scores, ('gr', 'gc'), split_axis=0, concat_axis=0, tiled=T...  10.3 us
    pallas_call x1, Pallas kernels, more_rows(): pl.pallas_call(kernel, in_specs=[VM, VM, VM], out_specs=[VM] * (3 * n), o...  7.87 us
    pallas_call x1, Pallas kernels, first_rows(): pl.pallas_call(kernel, in_specs=[VM], out_specs=[VM] * 5, out_shape=[jax....  5.25 us
    pallas_call x1, Pallas kernels, own_block(): pl.pallas_call(kernel, in_specs=[VM] * 6, out_specs=[HB, VM, VM], out_sha...  5.17 us
    all_to_all x1, starting transfers between devices, step(): lax.all_to_all(scores, ('gr', 'gc'), split_axis=0, concat_axis=0, tiled=T...  3.88 us
  transfers between devices with their start and end apart: 8, of which 2 were waited for; matrix products, arithmetic and copies ran while one was open for 0% of the time, Pallas kernels for 13%

profile of v3, /device:TPU:1, one launch (start us, length us, event | category | flops | bytes accessed | tf_op | source)
XLA Modules:
  0.0 105.1 jit_solution(5608327233180771569)
XLA Ops:
  0.6 10.6 %shard_map.50 = bf16[2048,768]{1,0:T(8,128)(2,1)} custom-call(s32[64,128]{1,0:T(8,128)} %bitcast.8, s32[1,128]{1,0:T(1,128)} %bitcast.9, bf16[8192,768]{1,0:T(8,128)(2,1)} %emb_ref.1), custom_call_target="tpu_custom_call" | custom-call | tf_op jit(solution)/shard_map/pallas_call | solution.py:171
  11.2 46.1 %all_to_all.10 = bf16[16,128,768]{2,1,0:T(8,128)(2,1)S(1)} all-to-all(bf16[16,128,768]{2,1,0:T(8,128)(2,1)} %bitcast.7), channel_id=1, replica_groups=mesh['ingest'=16,'gr'=4,'gc'=2] {'ingest'}, dimensions={0} | all-to-all | bytes 6291456 | tf_op jit(solution)/shard_map/all_to_all | solution.py:349
  57.3 5.3 %shard_map.51 = (bf16[2048,768]{1,0:T(8,128)(2,1)S(1)}, f32[8,2048]{1,0:T(8,128)S(1)}, bf16[512,384]{1,0:T(8,128)(2,1)S(1)}, bf16[512,384]{1,0:T(8,128)(2,1)S(1)}, f32[1,512]{1,0:T(1,128)S(1)}) custom-call(bf16[2048,768]{1,0:T(8,128)(2,1)S(1)} %bitcast.4), custom_call_target="tpu_custom_call" | custom-call | flops 3221225472 | bytes 6291456 | tf_op jit(solution)/shard_map/pallas_call | solution.py:255
  62.6 3.7 %collective-permute-start.4 = (bf16[512,384]{1,0:T(8,128)(2,1)S(1)}, bf16[512,384]{1,0:T(8,128)(2,1)S(1)}, u32[]{:S(2)}, u32[]{:S(2)}) collective-permute-start(bf16[512,384]{1,0:T(8,128)(2,1)S(1)} %get-tuple-element.22), channel_id=1, source_target_pairs={{0,4},{1,5},{2,6},{3,7},{4,0},{5,1},{6,2},{7,3},{8,12},{9,13},{10,... | collective-permute-start | bytes 1179656 | tf_op jit(solution)/shard_map/ppermute | solution.py:356
  66.3 2.0 %collective-permute-start.5 = (bf16[512,384]{1,0:T(8,128)(2,1)S(1)}, bf16[512,384]{1,0:T(8,128)(2,1)S(1)}, u32[]{:S(2)}, u32[]{:S(2)}) collective-permute-start(bf16[512,384]{1,0:T(8,128)(2,1)S(1)} %get-tuple-element.23), channel_id=1, source_target_pairs={{0,5},{1,4},{2,7},{3,6},{4,1},{5,0},{6,3},{7,2},{8,13},{9,12},{10,... | collective-permute-start | bytes 1179656 | tf_op jit(solution)/shard_map/ppermute | solution.py:356
  68.3 7.9 %shard_map.52 = (bf16[512,384]{1,0:T(8,128)(2,1)S(1)}, bf16[512,384]{1,0:T(8,128)(2,1)}, f32[1,512]{1,0:T(1,128)S(1)}, bf16[512,384]{1,0:T(8,128)(2,1)S(1)}, bf1...) custom-call(bf16[2048,768]{1,0:T(8,128)(2,1)S(1)} %bitcast.5, bf16[2048,768]{1,0:T(8,128)(2,1)S(1)} %get-tuple-element.16.normed, ...), custom_call_target="tpu_custom_call" | custom-call | flops 6442450944 | bytes 6291456 | tf_op jit(solution)/shard_map/pallas_call | solution.py:276
  76.2 0.9 collective-permute-start
  77.1 5.2 %shard_map.53 = (bf16[8,512,384]{2,1,0:T(8,128)(2,1)}, bf16[512,384]{1,0:T(8,128)(2,1)}, f32[8,1,512]{2,1,0:T(1,128)}) custom-call(bf16[2048,768]{1,0:T(8,128)(2,1)S(1)} %bitcast.6, bf16[2048,768]{1,0:T(8,128)(2,1)S(1)} %get-tuple-element.16.normed, f32[8,2048]{1,0:T(8,128)S(1)} %get-tuple-element.17.bias, f32[1,512]{1,0:T(1,128)S(1)} %get-tuple-element.24.c1, ...), custom_call_target="tpu_custom_call" | custom-call | flops 3221225472 | bytes 6291456 | tf_op jit(solution)/shard_map/pallas_call | solution.py:297
  82.3 0.7 collective-permute-start.6
  83.0 2.1 %collective-permute-start.1 = (bf16[512,384]{1,0:T(8,128)(2,1)}, bf16[512,384]{1,0:T(8,128)(2,1)S(1)}, u32[]{:S(2)}, u32[]{:S(2)}) collective-permute-start(bf16[512,384]{1,0:T(8,128)(2,1)} %get-tuple-element.19), channel_id=1, source_target_pairs={{0,7},{1,6},{2,1},{3,0},{4,3},{5,2},{6,5},{7,4},{8,15},{9,14},{10,... | collective-permute-start | bytes 1179656 | tf_op jit(solution)/shard_map/ppermute | solution.py:356
  85.2 0.0 collective-permute-done.4.refs_0_
  85.2 0.0 collective-permute-start.2
  85.2 1.1 %collective-permute-done.5.refs_1_ = bf16[512,384]{1,0:T(8,128)(2,1)S(1)} collective-permute-done((bf16[512,384]{1,0:T(8,128)(2,1)S(1)}, bf16[512,384]{1,0:T(8,128)(2,1)S(1)}, u32[]{:S(2)}, u32[]{:S(2)}) %collective-permute-start.5) | collective-permute-done | bytes 393248 | tf_op jit(solution)/shard_map/ppermute | solution.py:356
  86.3 1.5 %collective-permute-start.3 = (bf16[512,384]{1,0:T(8,128)(2,1)S(1)}, bf16[512,384]{1,0:T(8,128)(2,1)S(1)}, u32[]{:S(2)}, u32[]{:S(2)}) collective-permute-start(bf16[512,384]{1,0:T(8,128)(2,1)S(1)} %get-tuple-element.21), channel_id=1, source_target_pairs={{0,6},{1,7},{2,0},{3,1},{4,2},{5,3},{6,4},{7,5},{8,14},{9,15},{10,... | collective-permute-start | bytes 1179656 | tf_op jit(solution)/shard_map/ppermute | solution.py:356
  87.9 3.9 %all-to-all-start.1 = ((f32[8,1,512]{2,1,0:T(1,128)}), f32[8,1,512]{2,1,0:T(1,128)S(1)}, u32[]{:S(2)}, u32[]{:S(2)}) async-start(f32[8,1,512]{2,1,0:T(1,128)} %get-tuple-element.29), calls=%async_computation.1 | async-start | bytes 32768 | tf_op jit(solution)/shard_map/all_to_all | solution.py:364
  91.7 0.0 collective-permute-done.6.refs_2_
  91.7 1.0 shard_map.54.refs_4_
  92.8 10.3 %all-to-all-done.1.refs_5_ = f32[8,1,512]{2,1,0:T(1,128)S(1)} async-done(((f32[8,1,512]{2,1,0:T(1,128)}), f32[8,1,512]{2,1,0:T(1,128)S(1)}, u32[]{:S(2)}, u32[]{:S(2)}) %all-to-all-start.1) | async-done | bytes 16416 | tf_op jit(solution)/shard_map/all_to_all | solution.py:364
  103.1 0.0 collective-permute-done.refs_0_
  103.1 0.0 collective-permute-done.1.refs_1_
  103.1 0.0 collective-permute-done.2.refs_2_
  103.1 0.0 collective-permute-done.3.refs_3_
  103.1 1.8 %shard_map.55 = (bf16[8,512,384]{2,1,0:T(8,128)(2,1)}, f32[8,512]{1,0:T(8,128)}) custom-call(bf16[512,384]{1,0:T(8,128)(2,1)S(1)} %collective-permute-done.refs_0_, bf16[512,384]{1,0:T(8,128)(2,1)S(1)} %collective-permute-done.1.refs_1_, bf16[512,384]{1,0:T(8,128)(2,1)S(1)} %collective-permute-done.2.refs_2_, ...), custom_call_target="tpu_custom_call", output_to_operand_aliasing={{0}: (4, {})} | custom-call | tf_op jit(solution)/shard_map/pallas_call | solution.py:336
Async XLA Ops:
  62.6 22.6 %collective-permute-start.4 = (bf16[512,384]{1,0:T(8,128)(2,1)S(1)}, bf16[512,384]{1,0:T(8,128)(2,1)S(1)}, u32[]{:S(2)}, u32[]{:S(2)}) collective-permute-start(bf16[512,384]{1,0:T(8,128)(2,1)S(1)} %get-tuple-element.22), channel_id=1, source_target_pairs={{0,4},{1,5},{2,6},{3,7},{4,0},{5,1},{6,2},{7,3},{8,12},{9,13},{10,... | collective-permute-start | bytes 1179656 | tf_op jit(solution)/shard_map/ppermute | solution.py:356
  66.3 20.1 %collective-permute-start.5 = (bf16[512,384]{1,0:T(8,128)(2,1)S(1)}, bf16[512,384]{1,0:T(8,128)(2,1)S(1)}, u32[]{:S(2)}, u32[]{:S(2)}) collective-permute-start(bf16[512,384]{1,0:T(8,128)(2,1)S(1)} %get-tuple-element.23), channel_id=1, source_target_pairs={{0,5},{1,4},{2,7},{3,6},{4,1},{5,0},{6,3},{7,2},{8,13},{9,12},{10,... | collective-permute-start | bytes 1179656 | tf_op jit(solution)/shard_map/ppermute | solution.py:356
  76.2 26.9 %collective-permute-start = (bf16[512,384]{1,0:T(8,128)(2,1)}, bf16[512,384]{1,0:T(8,128)(2,1)S(1)}, u32[]{:S(2)}, u32[]{:S(2)}) collective-permute-start(bf16[512,384]{1,0:T(8,128)(2,1)} %get-tuple-element.18), channel_id=1, source_target_pairs={{0,3},{1,2},{2,5},{3,4},{4,7},{5,6},{6,1},{7,0},{8,11},{9,10},{10,... | collective-permute-start | bytes 1179656 | tf_op jit(solution)/shard_map/ppermute | solution.py:356
  82.3 9.4 %collective-permute-start.6 = (bf16[512,384]{1,0:T(8,128)(2,1)}, bf16[512,384]{1,0:T(8,128)(2,1)S(1)}, u32[]{:S(2)}, u32[]{:S(2)}) collective-permute-start(bf16[512,384]{1,0:T(8,128)(2,1)} %get-tuple-element.27), channel_id=1, source_target_pairs={{0,1},{1,0},{2,3},{3,2},{4,5},{5,4},{6,7},{7,6},{8,9},{9,8},{10,11... | collective-permute-start | bytes 1179656 | tf_op jit(solution)/shard_map/ppermute | solution.py:356
  83.0 20.0 %collective-permute-start.1 = (bf16[512,384]{1,0:T(8,128)(2,1)}, bf16[512,384]{1,0:T(8,128)(2,1)S(1)}, u32[]{:S(2)}, u32[]{:S(2)}) collective-permute-start(bf16[512,384]{1,0:T(8,128)(2,1)} %get-tuple-element.19), channel_id=1, source_target_pairs={{0,7},{1,6},{2,1},{3,0},{4,3},{5,2},{6,5},{7,4},{8,15},{9,14},{10,... | collective-permute-start | bytes 1179656 | tf_op jit(solution)/shard_map/ppermute | solution.py:356
  85.2 17.9 %collective-permute-start.2 = (bf16[512,384]{1,0:T(8,128)(2,1)S(1)}, bf16[512,384]{1,0:T(8,128)(2,1)S(1)}, u32[]{:S(2)}, u32[]{:S(2)}) collective-permute-start(bf16[512,384]{1,0:T(8,128)(2,1)S(1)} %get-tuple-element.20), channel_id=1, source_target_pairs={{0,2},{1,3},{2,4},{3,5},{4,6},{5,7},{6,0},{7,1},{8,10},{9,11},{10,... | collective-permute-start | bytes 1179656 | tf_op jit(solution)/shard_map/ppermute | solution.py:356
  86.3 16.8 %collective-permute-start.3 = (bf16[512,384]{1,0:T(8,128)(2,1)S(1)}, bf16[512,384]{1,0:T(8,128)(2,1)S(1)}, u32[]{:S(2)}, u32[]{:S(2)}) collective-permute-start(bf16[512,384]{1,0:T(8,128)(2,1)S(1)} %get-tuple-element.21), channel_id=1, source_target_pairs={{0,6},{1,7},{2,0},{3,1},{4,2},{5,3},{6,4},{7,5},{8,14},{9,15},{10,... | collective-permute-start | bytes 1179656 | tf_op jit(solution)/shard_map/ppermute | solution.py:356
  87.9 15.2 %all-to-all-start.1 = ((f32[8,1,512]{2,1,0:T(1,128)}), f32[8,1,512]{2,1,0:T(1,128)S(1)}, u32[]{:S(2)}, u32[]{:S(2)}) async-start(f32[8,1,512]{2,1,0:T(1,128)} %get-tuple-element.29), calls=%async_computation.1 | async-start | bytes 32768 | tf_op jit(solution)/shard_map/all_to_all | solution.py:364

commit v4 on v3

--- a/solution.py
+++ b/solution.py
@@ -22,7 +22,7 @@
 
 ROWS = 8192
 CH = ROWS // 128
-NSEG = 8
+NSEG = 4
 NL = 4
 GL = 16 // NL
 W = 48
@@ -108,12 +108,11 @@
         k = l * CH + 2 * i
         return jnp.concatenate([gref[pl.ds(k, 1), :], gref[pl.ds(k + 1, 1), :]], axis=1)
 
-    UN = 4
-    steps = seg // 256 // UN
+    UN = 8
     for s in range(NSEG):
         cps[s].wait()
 
-        def body(j, _):
+        def body(j):
             for u in range(UN):
                 i = j * UN + u
                 x = emb_v[pl.ds(pl.multiple_of(i * 256, 256), 256), :]
@@ -126,7 +125,7 @@
                     C[l, pl.ds(st[l], W), :] = C[l, pl.ds(st[l], W), :] + y[l * W : (l + 1) * W]
             return 0
 
-        lax.fori_loop(s * steps, (s + 1) * steps, body, 0)
+        body(s)
 
     def rest(i, _):
         for l in range(NL):
@@ -358,11 +357,13 @@
     normed, bias, k2, s2, c2 = first_rows(x)
     got = [send(k2, 2, 0), send(s2, 2, 1)]
     k1, s1, c1, k3, s3, c3 = more_rows(x, normed, bias, [(1, 0, BQ), (3, 0, BQ)])
-    last = [send(s1, 1, 1), send(s3, 3, 1), send(k1, 1, 0), send(k3, 3, 0)]
+    near = [send(s1, 1, 1), send(s3, 3, 1)]
+    last = [send(k1, 1, 0), send(k3, 3, 0)]
     out, s0, scores = own_block(x, normed, bias, (c1, c2, c3))
     got += [send(s0, 0, 1)]
     scores = lax.all_to_all(scores, ("gr", "gc"), split_axis=0, concat_axis=0, tiled=True)
     (out,) = place(out, got)
+    (out,) = place(out, near)
     return tuple(place(out, last, scores))
 
 

time: 105 us -> 104 us (level)
    all_to_all x1, waiting for transfers between devices: 10.3 us -> 7.19 us  [step(): lax.all_to_all(scores, ('gr', 'gc'), split_axis=0, concat_axis=0, tiled=T...]
    ppermute x7, waiting for transfers between devices: 1.14 us -> 3.33 us  [send(): return (dz, dc, start, lax.ppermute(a, ('gr', 'gc'), pairs))]
    pallas_call x2 -> x3, Pallas kernels: 2.82 us -> 3.43 us  [place(): pl.pallas_call(kernel, in_specs=[VM] * n + [HB] + [VM] * k, out_specs=[HB...]
  transfers between devices with their start and end apart: 8 -> 8, of which waited for: 2 -> 3; matrix products, arithmetic and copies ran while one was open for 0% -> 0% of each run, Pallas kernels for 13% -> 14%
where the time goes in v4:
time: 104 us
  blocking collectives  46.1 us (44%)
  Pallas kernels  31.7 us (30%)
  starting transfers between devices  14.9 us (14%)
  waiting for transfers between devices  10.5 us (10%)
    all_to_all x1, blocking collectives, step(): lax.all_to_all(outgoing.reshape(16, PR, D), 'ingest', split_axis=0, conca...  46.1 us
    ppermute x7, starting transfers between devices, send(): return (dz, dc, start, lax.ppermute(a, ('gr', 'gc'), pairs))  11.1 us
    pallas_call x1, Pallas kernels, gather(): pl.pallas_call(gk, in_specs=[pl.BlockSpec(memory_space=pltpu.VMEM), pl.Bl...  9.94 us
    pallas_call x1, Pallas kernels, more_rows(): pl.pallas_call(kernel, in_specs=[VM, VM, VM], out_specs=[VM] * (3 * n), o...  7.87 us
    all_to_all x1, waiting for transfers between devices, step(): lax.all_to_all(scores, ('gr', 'gc'), split_axis=0, concat_axis=0, tiled=T...  7.19 us
    pallas_call x1, Pallas kernels, first_rows(): pl.pallas_call(kernel, in_specs=[VM], out_specs=[VM] * 5, out_shape=[jax....  5.26 us
    pallas_call x1, Pallas kernels, own_block(): pl.pallas_call(kernel, in_specs=[VM] * 6, out_specs=[HB, VM, VM], out_sha...  5.17 us
    all_to_all x1, starting transfers between devices, step(): lax.all_to_all(scores, ('gr', 'gc'), split_axis=0, concat_axis=0, tiled=T...  3.88 us
  transfers between devices with their start and end apart: 8, of which 3 were waited for; matrix products, arithmetic and copies ran while one was open for 0% of the time, Pallas kernels for 14%

profile of v4, /device:TPU:1, one launch (start us, length us, event | category | flops | bytes accessed | tf_op | source)
XLA Modules:
  0.0 104.1 jit_solution(11341093211887968609)
XLA Ops:
  0.6 9.9 %shard_map.50 = bf16[2048,768]{1,0:T(8,128)(2,1)} custom-call(s32[64,128]{1,0:T(8,128)} %bitcast.8, s32[1,128]{1,0:T(1,128)} %bitcast.9, bf16[8192,768]{1,0:T(8,128)(2,1)} %emb_ref.1), custom_call_target="tpu_custom_call" | custom-call | tf_op jit(solution)/shard_map/pallas_call | solution.py:170
  10.6 46.1 %all_to_all.10 = bf16[16,128,768]{2,1,0:T(8,128)(2,1)S(1)} all-to-all(bf16[16,128,768]{2,1,0:T(8,128)(2,1)} %bitcast.7), channel_id=1, replica_groups=mesh['ingest'=16,'gr'=4,'gc'=2] {'ingest'}, dimensions={0} | all-to-all | bytes 6291456 | tf_op jit(solution)/shard_map/all_to_all | solution.py:348
  56.7 5.3 %shard_map.51 = (bf16[2048,768]{1,0:T(8,128)(2,1)S(1)}, f32[8,2048]{1,0:T(8,128)S(1)}, bf16[512,384]{1,0:T(8,128)(2,1)S(1)}, bf16[512,384]{1,0:T(8,128)(2,1)S(1)}, f32[1,512]{1,0:T(1,128)S(1)}) custom-call(bf16[2048,768]{1,0:T(8,128)(2,1)S(1)} %bitcast.4), custom_call_target="tpu_custom_call" | custom-call | flops 3221225472 | bytes 6291456 | tf_op jit(solution)/shard_map/pallas_call | solution.py:254
  61.9 3.6 %collective-permute-start.4 = (bf16[512,384]{1,0:T(8,128)(2,1)S(1)}, bf16[512,384]{1,0:T(8,128)(2,1)S(1)}, u32[]{:S(2)}, u32[]{:S(2)}) collective-permute-start(bf16[512,384]{1,0:T(8,128)(2,1)S(1)} %get-tuple-element.22), channel_id=1, source_target_pairs={{0,4},{1,5},{2,6},{3,7},{4,0},{5,1},{6,2},{7,3},{8,12},{9,13},{10,... | collective-permute-start | bytes 1179656 | tf_op jit(solution)/shard_map/ppermute | solution.py:355
  65.6 2.1 %collective-permute-start.5 = (bf16[512,384]{1,0:T(8,128)(2,1)S(1)}, bf16[512,384]{1,0:T(8,128)(2,1)S(1)}, u32[]{:S(2)}, u32[]{:S(2)}) collective-permute-start(bf16[512,384]{1,0:T(8,128)(2,1)S(1)} %get-tuple-element.23), channel_id=1, source_target_pairs={{0,5},{1,4},{2,7},{3,6},{4,1},{5,0},{6,3},{7,2},{8,13},{9,12},{10,... | collective-permute-start | bytes 1179656 | tf_op jit(solution)/shard_map/ppermute | solution.py:355
  67.6 7.9 %shard_map.52 = (bf16[512,384]{1,0:T(8,128)(2,1)S(1)}, bf16[512,384]{1,0:T(8,128)(2,1)}, f32[1,512]{1,0:T(1,128)S(1)}, bf16[512,384]{1,0:T(8,128)(2,1)S(1)}, bf1...) custom-call(bf16[2048,768]{1,0:T(8,128)(2,1)S(1)} %bitcast.5, bf16[2048,768]{1,0:T(8,128)(2,1)S(1)} %get-tuple-element.16.normed, ...), custom_call_target="tpu_custom_call" | custom-call | flops 6442450944 | bytes 6291456 | tf_op jit(solution)/shard_map/pallas_call | solution.py:275
  75.5 1.0 collective-permute-start.2
  76.5 5.2 %shard_map.53 = (bf16[8,512,384]{2,1,0:T(8,128)(2,1)}, bf16[512,384]{1,0:T(8,128)(2,1)}, f32[8,1,512]{2,1,0:T(1,128)}) custom-call(bf16[2048,768]{1,0:T(8,128)(2,1)S(1)} %bitcast.6, bf16[2048,768]{1,0:T(8,128)(2,1)S(1)} %get-tuple-element.16.normed, f32[8,2048]{1,0:T(8,128)S(1)} %get-tuple-element.17.bias, f32[1,512]{1,0:T(1,128)S(1)} %get-tuple-element.24.c1, ...), custom_call_target="tpu_custom_call" | custom-call | flops 3221225472 | bytes 6291456 | tf_op jit(solution)/shard_map/pallas_call | solution.py:296
  81.6 0.7 collective-permute-start.6
  82.4 2.1 %collective-permute-start.3 = (bf16[512,384]{1,0:T(8,128)(2,1)}, bf16[512,384]{1,0:T(8,128)(2,1)S(1)}, u32[]{:S(2)}, u32[]{:S(2)}) collective-permute-start(bf16[512,384]{1,0:T(8,128)(2,1)} %get-tuple-element.21), channel_id=1, source_target_pairs={{0,7},{1,6},{2,1},{3,0},{4,3},{5,2},{6,5},{7,4},{8,15},{9,14},{10,... | collective-permute-start | bytes 1179656 | tf_op jit(solution)/shard_map/ppermute | solution.py:355
  84.5 0.0 collective-permute-done.4.refs_0_
  84.5 0.0 collective-permute-start
  84.5 1.1 %collective-permute-done.5.refs_1_ = bf16[512,384]{1,0:T(8,128)(2,1)S(1)} collective-permute-done((bf16[512,384]{1,0:T(8,128)(2,1)S(1)}, bf16[512,384]{1,0:T(8,128)(2,1)S(1)}, u32[]{:S(2)}, u32[]{:S(2)}) %collective-permute-start.5) | collective-permute-done | bytes 393248 | tf_op jit(solution)/shard_map/ppermute | solution.py:355
  85.6 1.5 %collective-permute-start.1 = (bf16[512,384]{1,0:T(8,128)(2,1)S(1)}, bf16[512,384]{1,0:T(8,128)(2,1)S(1)}, u32[]{:S(2)}, u32[]{:S(2)}) collective-permute-start(bf16[512,384]{1,0:T(8,128)(2,1)S(1)} %get-tuple-element.19), channel_id=1, source_target_pairs={{0,6},{1,7},{2,0},{3,1},{4,2},{5,3},{6,4},{7,5},{8,14},{9,15},{10,... | collective-permute-start | bytes 1179656 | tf_op jit(solution)/shard_map/ppermute | solution.py:355
  87.2 3.9 %all-to-all-start.1 = ((f32[8,1,512]{2,1,0:T(1,128)}), f32[8,1,512]{2,1,0:T(1,128)S(1)}, u32[]{:S(2)}, u32[]{:S(2)}) async-start(f32[8,1,512]{2,1,0:T(1,128)} %get-tuple-element.29), calls=%async_computation.1 | async-start | bytes 32768 | tf_op jit(solution)/shard_map/all_to_all | solution.py:364
  91.1 0.0 collective-permute-done.6.refs_2_
  91.1 1.0 shard_map.54.refs_2_
  92.1 0.0 collective-permute-done.2.refs_0_
  92.1 2.2 %collective-permute-done.3.refs_1_ = bf16[512,384]{1,0:T(8,128)(2,1)S(1)} collective-permute-done((bf16[512,384]{1,0:T(8,128)(2,1)}, bf16[512,384]{1,0:T(8,128)(2,1)S(1)}, u32[]{:S(2)}, u32[]{:S(2)}) %collective-permute-start.3) | collective-permute-done | bytes 393248 | tf_op jit(solution)/shard_map/ppermute | solution.py:355
  94.3 0.9 shard_map.55.refs_2_
  95.2 7.2 %all-to-all-done.1.refs_3_ = f32[8,1,512]{2,1,0:T(1,128)S(1)} async-done(((f32[8,1,512]{2,1,0:T(1,128)}), f32[8,1,512]{2,1,0:T(1,128)S(1)}, u32[]{:S(2)}, u32[]{:S(2)}) %all-to-all-start.1) | async-done | bytes 16416 | tf_op jit(solution)/shard_map/all_to_all | solution.py:364
  102.4 0.0 collective-permute-done.refs_0_
  102.4 0.0 collective-permute-done.1.refs_1_
  102.4 1.5 %shard_map.56 = (bf16[8,512,384]{2,1,0:T(8,128)(2,1)}, f32[8,512]{1,0:T(8,128)}) custom-call(bf16[512,384]{1,0:T(8,128)(2,1)S(1)} %collective-permute-done.refs_0_, bf16[512,384]{1,0:T(8,128)(2,1)S(1)} %collective-permute-done.1.refs_1_, bf16[8,512,384]{2,1,0:T(8,128)(2,1)} %shard_map.55.refs_2_, ...), custom_call_target="tpu_custom_call", output_to_operand_aliasing={{0}: (2, {})} | custom-call | tf_op jit(solution)/shard_map/pallas_call | solution.py:335
Async XLA Ops:
  61.9 22.6 %collective-permute-start.4 = (bf16[512,384]{1,0:T(8,128)(2,1)S(1)}, bf16[512,384]{1,0:T(8,128)(2,1)S(1)}, u32[]{:S(2)}, u32[]{:S(2)}) collective-permute-start(bf16[512,384]{1,0:T(8,128)(2,1)S(1)} %get-tuple-element.22), channel_id=1, source_target_pairs={{0,4},{1,5},{2,6},{3,7},{4,0},{5,1},{6,2},{7,3},{8,12},{9,13},{10,... | collective-permute-start | bytes 1179656 | tf_op jit(solution)/shard_map/ppermute | solution.py:355
  65.6 20.1 %collective-permute-start.5 = (bf16[512,384]{1,0:T(8,128)(2,1)S(1)}, bf16[512,384]{1,0:T(8,128)(2,1)S(1)}, u32[]{:S(2)}, u32[]{:S(2)}) collective-permute-start(bf16[512,384]{1,0:T(8,128)(2,1)S(1)} %get-tuple-element.23), channel_id=1, source_target_pairs={{0,5},{1,4},{2,7},{3,6},{4,1},{5,0},{6,3},{7,2},{8,13},{9,12},{10,... | collective-permute-start | bytes 1179656 | tf_op jit(solution)/shard_map/ppermute | solution.py:355
  75.5 16.6 %collective-permute-start.2 = (bf16[512,384]{1,0:T(8,128)(2,1)}, bf16[512,384]{1,0:T(8,128)(2,1)S(1)}, u32[]{:S(2)}, u32[]{:S(2)}) collective-permute-start(bf16[512,384]{1,0:T(8,128)(2,1)} %get-tuple-element.20), channel_id=1, source_target_pairs={{0,3},{1,2},{2,5},{3,4},{4,7},{5,6},{6,1},{7,0},{8,11},{9,10},{10,... | collective-permute-start | bytes 1179656 | tf_op jit(solution)/shard_map/ppermute | solution.py:355
  81.6 9.4 %collective-permute-start.6 = (bf16[512,384]{1,0:T(8,128)(2,1)}, bf16[512,384]{1,0:T(8,128)(2,1)S(1)}, u32[]{:S(2)}, u32[]{:S(2)}) collective-permute-start(bf16[512,384]{1,0:T(8,128)(2,1)} %get-tuple-element.27), channel_id=1, source_target_pairs={{0,1},{1,0},{2,3},{3,2},{4,5},{5,4},{6,7},{7,6},{8,9},{9,8},{10,11... | collective-permute-start | bytes 1179656 | tf_op jit(solution)/shard_map/ppermute | solution.py:355
  82.4 11.9 %collective-permute-start.3 = (bf16[512,384]{1,0:T(8,128)(2,1)}, bf16[512,384]{1,0:T(8,128)(2,1)S(1)}, u32[]{:S(2)}, u32[]{:S(2)}) collective-permute-start(bf16[512,384]{1,0:T(8,128)(2,1)} %get-tuple-element.21), channel_id=1, source_target_pairs={{0,7},{1,6},{2,1},{3,0},{4,3},{5,2},{6,5},{7,4},{8,15},{9,14},{10,... | collective-permute-start | bytes 1179656 | tf_op jit(solution)/shard_map/ppermute | solution.py:355
  84.5 17.9 %collective-permute-start = (bf16[512,384]{1,0:T(8,128)(2,1)S(1)}, bf16[512,384]{1,0:T(8,128)(2,1)S(1)}, u32[]{:S(2)}, u32[]{:S(2)}) collective-permute-start(bf16[512,384]{1,0:T(8,128)(2,1)S(1)} %get-tuple-element.18), channel_id=1, source_target_pairs={{0,2},{1,3},{2,4},{3,5},{4,6},{5,7},{6,0},{7,1},{8,10},{9,11},{10,... | collective-permute-start | bytes 1179656 | tf_op jit(solution)/shard_map/ppermute | solution.py:355
  85.6 16.8 %collective-permute-start.1 = (bf16[512,384]{1,0:T(8,128)(2,1)S(1)}, bf16[512,384]{1,0:T(8,128)(2,1)S(1)}, u32[]{:S(2)}, u32[]{:S(2)}) collective-permute-start(bf16[512,384]{1,0:T(8,128)(2,1)S(1)} %get-tuple-element.19), channel_id=1, source_target_pairs={{0,6},{1,7},{2,0},{3,1},{4,2},{5,3},{6,4},{7,5},{8,14},{9,15},{10,... | collective-permute-start | bytes 1179656 | tf_op jit(solution)/shard_map/ppermute | solution.py:355
  87.2 15.2 %all-to-all-start.1 = ((f32[8,1,512]{2,1,0:T(1,128)}), f32[8,1,512]{2,1,0:T(1,128)S(1)}, u32[]{:S(2)}, u32[]{:S(2)}) async-start(f32[8,1,512]{2,1,0:T(1,128)} %get-tuple-element.29), calls=%async_computation.1 | async-start | bytes 32768 | tf_op jit(solution)/shard_map/all_to_all | solution.py:364

commit v5 on v4

--- a/solution.py
+++ b/solution.py
@@ -48,8 +48,10 @@
     hotb = hot.astype(bf16).reshape(CH * 16, 128)
     upper = (iota((128, 128), 0) < iota((128, 128), 1)).astype(bf16)
     ones = jnp.ones((128, 128), bf16)
-    pre = dot(hotb, upper).reshape(CH, 16, 128)
-    tot = dot(hotb, ones).reshape(CH, 16, 128)
+    both = jnp.concatenate([upper, ones], axis=1)
+    sums = dot(hotb, both)
+    pre = sums[:, :128].reshape(CH, 16, 128)
+    tot = sums[:, 128:].reshape(CH, 16, 128)
     carry = jnp.ones((16, 128), f32)
     for a in range(CH):
         rk[a] = carry + pre[a]
@@ -64,8 +66,8 @@
     rr = iota((NL * CH, NL * CH), 0)
     cc = iota((NL * CH, NL * CH), 1)
     lower = (((rr >> 6) == (cc >> 6)) & (cc < rr)).astype(bf16)
-    tb = dot(vb, ones).astype(bf16)
-    g = dot(lower, tb) + dot(vb, upper)
+    vsums = dot(vb, both)
+    g = dot(lower, vsums[:, 128:].astype(bf16)) + vsums[:, :128]
     gref[...] = jnp.where(valid, g, -1e6).astype(jnp.int32)
     trow = dot(jnp.ones((8, 128), bf16), vb, NT).astype(bf16)
     before = (iota((CH, 128), 0) < iota((CH, 128), 1)).astype(bf16)
@@ -247,8 +249,8 @@
             v = x_ref[s, :].astype(f32)
             sq = jnp.sum(v * v, axis=1, keepdims=True)
             normed[s, :] = (v * lax.rsqrt(sq + 1e-6)).astype(bf16)
-        e0 = (iota((8, D), 1) == 0).astype(bf16)
-        bias[...] = jnp.where(dot(e0, x_ref[...], NT) > 32.0, -1e30, -8.0 * LOG2E)
+        e0 = (iota((8, 128), 1) == 0).astype(bf16)
+        bias[...] = jnp.where(dot(e0, x_ref[:, 0:128], NT) > 32.0, -1e30, -8.0 * LOG2E)
         query_rows(rows_of(position()[0] + 2, 0, 512), x_ref, normed, bias, *outs)
 
     return pl.pallas_call(

time: 104 us -> 104 us (level)
  no operation moved by 1% of the time
where the time goes in v5:
time: 104 us
  blocking collectives  46.1 us (44%)
  Pallas kernels  31.4 us (30%)
  starting transfers between devices  14.9 us (14%)
  waiting for transfers between devices  10.5 us (10%)
    all_to_all x1, blocking collectives, step(): lax.all_to_all(outgoing.reshape(16, PR, D), 'ingest', split_axis=0, conca...  46.1 us
    ppermute x7, starting transfers between devices, send(): return (dz, dc, start, lax.ppermute(a, ('gr', 'gc'), pairs))  11.1 us
    pallas_call x1, Pallas kernels, gather(): pl.pallas_call(gk, in_specs=[pl.BlockSpec(memory_space=pltpu.VMEM), pl.Bl...  10 us
    pallas_call x1, Pallas kernels, more_rows(): pl.pallas_call(kernel, in_specs=[VM, VM, VM], out_specs=[VM] * (3 * n), o...  7.87 us
    all_to_all x1, waiting for transfers between devices, step(): lax.all_to_all(scores, ('gr', 'gc'), split_axis=0, concat_axis=0, tiled=T...  7.19 us
    pallas_call x1, Pallas kernels, own_block(): pl.pallas_call(kernel, in_specs=[VM] * 6, out_specs=[HB, VM, VM], out_sha...  5.17 us
    pallas_call x1, Pallas kernels, first_rows(): pl.pallas_call(kernel, in_specs=[VM], out_specs=[VM] * 5, out_shape=[jax....  4.91 us
    all_to_all x1, starting transfers between devices, step(): lax.all_to_all(scores, ('gr', 'gc'), split_axis=0, concat_axis=0, tiled=T...  3.88 us
  transfers between devices with their start and end apart: 8, of which 3 were waited for; matrix products, arithmetic and copies ran while one was open for 0% of the time, Pallas kernels for 14%

profile of v5, /device:TPU:1, one launch (start us, length us, event | category | flops | bytes accessed | tf_op | source)
XLA Modules:
  0.0 103.8 jit_solution(17061857306586254129)
XLA Ops:
  0.6 10.0 %shard_map.50 = bf16[2048,768]{1,0:T(8,128)(2,1)} custom-call(s32[64,128]{1,0:T(8,128)} %bitcast.8, s32[1,128]{1,0:T(1,128)} %bitcast.9, bf16[8192,768]{1,0:T(8,128)(2,1)} %emb_ref.1), custom_call_target="tpu_custom_call" | custom-call | tf_op jit(solution)/shard_map/pallas_call | solution.py:172
  10.7 46.1 %all_to_all.10 = bf16[16,128,768]{2,1,0:T(8,128)(2,1)S(1)} all-to-all(bf16[16,128,768]{2,1,0:T(8,128)(2,1)} %bitcast.7), channel_id=1, replica_groups=mesh['ingest'=16,'gr'=4,'gc'=2] {'ingest'}, dimensions={0} | all-to-all | bytes 6291456 | tf_op jit(solution)/shard_map/all_to_all | solution.py:350
  56.8 4.9 %shard_map.51 = (bf16[2048,768]{1,0:T(8,128)(2,1)S(1)}, f32[8,2048]{1,0:T(8,128)S(1)}, bf16[512,384]{1,0:T(8,128)(2,1)S(1)}, bf16[512,384]{1,0:T(8,128)(2,1)S(1)}, f32[1,512]{1,0:T(1,128)S(1)}) custom-call(bf16[2048,768]{1,0:T(8,128)(2,1)S(1)} %bitcast.4), custom_call_target="tpu_custom_call" | custom-call | flops 3221225472 | bytes 6291456 | tf_op jit(solution)/shard_map/pallas_call | solution.py:256
  61.7 3.6 %collective-permute-start.4 = (bf16[512,384]{1,0:T(8,128)(2,1)S(1)}, bf16[512,384]{1,0:T(8,128)(2,1)S(1)}, u32[]{:S(2)}, u32[]{:S(2)}) collective-permute-start(bf16[512,384]{1,0:T(8,128)(2,1)S(1)} %get-tuple-element.22), channel_id=1, source_target_pairs={{0,4},{1,5},{2,6},{3,7},{4,0},{5,1},{6,2},{7,3},{8,12},{9,13},{10,... | collective-permute-start | bytes 1179656 | tf_op jit(solution)/shard_map/ppermute | solution.py:357
  65.3 2.1 %collective-permute-start.5 = (bf16[512,384]{1,0:T(8,128)(2,1)S(1)}, bf16[512,384]{1,0:T(8,128)(2,1)S(1)}, u32[]{:S(2)}, u32[]{:S(2)}) collective-permute-start(bf16[512,384]{1,0:T(8,128)(2,1)S(1)} %get-tuple-element.23), channel_id=1, source_target_pairs={{0,5},{1,4},{2,7},{3,6},{4,1},{5,0},{6,3},{7,2},{8,13},{9,12},{10,... | collective-permute-start | bytes 1179656 | tf_op jit(solution)/shard_map/ppermute | solution.py:357
  67.4 7.9 %shard_map.52 = (bf16[512,384]{1,0:T(8,128)(2,1)S(1)}, bf16[512,384]{1,0:T(8,128)(2,1)}, f32[1,512]{1,0:T(1,128)S(1)}, bf16[512,384]{1,0:T(8,128)(2,1)S(1)}, bf1...) custom-call(bf16[2048,768]{1,0:T(8,128)(2,1)S(1)} %bitcast.5, bf16[2048,768]{1,0:T(8,128)(2,1)S(1)} %get-tuple-element.16.normed, ...), custom_call_target="tpu_custom_call" | custom-call | flops 6442450944 | bytes 6291456 | tf_op jit(solution)/shard_map/pallas_call | solution.py:277
  75.3 1.0 collective-permute-start.2
  76.2 5.2 %shard_map.53 = (bf16[8,512,384]{2,1,0:T(8,128)(2,1)}, bf16[512,384]{1,0:T(8,128)(2,1)}, f32[8,1,512]{2,1,0:T(1,128)}) custom-call(bf16[2048,768]{1,0:T(8,128)(2,1)S(1)} %bitcast.6, bf16[2048,768]{1,0:T(8,128)(2,1)S(1)} %get-tuple-element.16.normed, f32[8,2048]{1,0:T(8,128)S(1)} %get-tuple-element.17.bias, f32[1,512]{1,0:T(1,128)S(1)} %get-tuple-element.24.c1, ...), custom_call_target="tpu_custom_call" | custom-call | flops 3221225472 | bytes 6291456 | tf_op jit(solution)/shard_map/pallas_call | solution.py:298
  81.4 0.7 collective-permute-start.6
  82.1 2.1 %collective-permute-start.3 = (bf16[512,384]{1,0:T(8,128)(2,1)}, bf16[512,384]{1,0:T(8,128)(2,1)S(1)}, u32[]{:S(2)}, u32[]{:S(2)}) collective-permute-start(bf16[512,384]{1,0:T(8,128)(2,1)} %get-tuple-element.21), channel_id=1, source_target_pairs={{0,7},{1,6},{2,1},{3,0},{4,3},{5,2},{6,5},{7,4},{8,15},{9,14},{10,... | collective-permute-start | bytes 1179656 | tf_op jit(solution)/shard_map/ppermute | solution.py:357
  84.3 0.0 collective-permute-done.4.refs_0_
  84.3 0.0 collective-permute-start
  84.3 1.1 %collective-permute-done.5.refs_1_ = bf16[512,384]{1,0:T(8,128)(2,1)S(1)} collective-permute-done((bf16[512,384]{1,0:T(8,128)(2,1)S(1)}, bf16[512,384]{1,0:T(8,128)(2,1)S(1)}, u32[]{:S(2)}, u32[]{:S(2)}) %collective-permute-start.5) | collective-permute-done | bytes 393248 | tf_op jit(solution)/shard_map/ppermute | solution.py:357
  85.4 1.6 %collective-permute-start.1 = (bf16[512,384]{1,0:T(8,128)(2,1)S(1)}, bf16[512,384]{1,0:T(8,128)(2,1)S(1)}, u32[]{:S(2)}, u32[]{:S(2)}) collective-permute-start(bf16[512,384]{1,0:T(8,128)(2,1)S(1)} %get-tuple-element.19), channel_id=1, source_target_pairs={{0,6},{1,7},{2,0},{3,1},{4,2},{5,3},{6,4},{7,5},{8,14},{9,15},{10,... | collective-permute-start | bytes 1179656 | tf_op jit(solution)/shard_map/ppermute | solution.py:357
  86.9 3.9 %all-to-all-start.1 = ((f32[8,1,512]{2,1,0:T(1,128)}), f32[8,1,512]{2,1,0:T(1,128)S(1)}, u32[]{:S(2)}, u32[]{:S(2)}) async-start(f32[8,1,512]{2,1,0:T(1,128)} %get-tuple-element.29), calls=%async_computation.1 | async-start | bytes 32768 | tf_op jit(solution)/shard_map/all_to_all | solution.py:366
  90.8 0.0 collective-permute-done.6.refs_2_
  90.8 1.0 shard_map.54.refs_2_
  91.9 0.0 collective-permute-done.2.refs_0_
  91.9 2.2 %collective-permute-done.3.refs_1_ = bf16[512,384]{1,0:T(8,128)(2,1)S(1)} collective-permute-done((bf16[512,384]{1,0:T(8,128)(2,1)}, bf16[512,384]{1,0:T(8,128)(2,1)S(1)}, u32[]{:S(2)}, u32[]{:S(2)}) %collective-permute-start.3) | collective-permute-done | bytes 393248 | tf_op jit(solution)/shard_map/ppermute | solution.py:357
  94.1 0.9 shard_map.55.refs_2_
  95.0 7.2 %all-to-all-done.1.refs_3_ = f32[8,1,512]{2,1,0:T(1,128)S(1)} async-done(((f32[8,1,512]{2,1,0:T(1,128)}), f32[8,1,512]{2,1,0:T(1,128)S(1)}, u32[]{:S(2)}, u32[]{:S(2)}) %all-to-all-start.1) | async-done | bytes 16416 | tf_op jit(solution)/shard_map/all_to_all | solution.py:366
  102.1 0.0 collective-permute-done.refs_0_
  102.1 0.0 collective-permute-done.1.refs_1_
  102.2 1.5 %shard_map.56 = (bf16[8,512,384]{2,1,0:T(8,128)(2,1)}, f32[8,512]{1,0:T(8,128)}) custom-call(bf16[512,384]{1,0:T(8,128)(2,1)S(1)} %collective-permute-done.refs_0_, bf16[512,384]{1,0:T(8,128)(2,1)S(1)} %collective-permute-done.1.refs_1_, bf16[8,512,384]{2,1,0:T(8,128)(2,1)} %shard_map.55.refs_2_, ...), custom_call_target="tpu_custom_call", output_to_operand_aliasing={{0}: (2, {})} | custom-call | tf_op jit(solution)/shard_map/pallas_call | solution.py:337
Async XLA Ops:
  61.7 22.6 %collective-permute-start.4 = (bf16[512,384]{1,0:T(8,128)(2,1)S(1)}, bf16[512,384]{1,0:T(8,128)(2,1)S(1)}, u32[]{:S(2)}, u32[]{:S(2)}) collective-permute-start(bf16[512,384]{1,0:T(8,128)(2,1)S(1)} %get-tuple-element.22), channel_id=1, source_target_pairs={{0,4},{1,5},{2,6},{3,7},{4,0},{5,1},{6,2},{7,3},{8,12},{9,13},{10,... | collective-permute-start | bytes 1179656 | tf_op jit(solution)/shard_map/ppermute | solution.py:357
  65.3 20.1 %collective-permute-start.5 = (bf16[512,384]{1,0:T(8,128)(2,1)S(1)}, bf16[512,384]{1,0:T(8,128)(2,1)S(1)}, u32[]{:S(2)}, u32[]{:S(2)}) collective-permute-start(bf16[512,384]{1,0:T(8,128)(2,1)S(1)} %get-tuple-element.23), channel_id=1, source_target_pairs={{0,5},{1,4},{2,7},{3,6},{4,1},{5,0},{6,3},{7,2},{8,13},{9,12},{10,... | collective-permute-start | bytes 1179656 | tf_op jit(solution)/shard_map/ppermute | solution.py:357
  75.3 16.6 %collective-permute-start.2 = (bf16[512,384]{1,0:T(8,128)(2,1)}, bf16[512,384]{1,0:T(8,128)(2,1)S(1)}, u32[]{:S(2)}, u32[]{:S(2)}) collective-permute-start(bf16[512,384]{1,0:T(8,128)(2,1)} %get-tuple-element.20), channel_id=1, source_target_pairs={{0,3},{1,2},{2,5},{3,4},{4,7},{5,6},{6,1},{7,0},{8,11},{9,10},{10,... | collective-permute-start | bytes 1179656 | tf_op jit(solution)/shard_map/ppermute | solution.py:357
  81.4 9.4 %collective-permute-start.6 = (bf16[512,384]{1,0:T(8,128)(2,1)}, bf16[512,384]{1,0:T(8,128)(2,1)S(1)}, u32[]{:S(2)}, u32[]{:S(2)}) collective-permute-start(bf16[512,384]{1,0:T(8,128)(2,1)} %get-tuple-element.27), channel_id=1, source_target_pairs={{0,1},{1,0},{2,3},{3,2},{4,5},{5,4},{6,7},{7,6},{8,9},{9,8},{10,11... | collective-permute-start | bytes 1179656 | tf_op jit(solution)/shard_map/ppermute | solution.py:357
  82.1 11.9 %collective-permute-start.3 = (bf16[512,384]{1,0:T(8,128)(2,1)}, bf16[512,384]{1,0:T(8,128)(2,1)S(1)}, u32[]{:S(2)}, u32[]{:S(2)}) collective-permute-start(bf16[512,384]{1,0:T(8,128)(2,1)} %get-tuple-element.21), channel_id=1, source_target_pairs={{0,7},{1,6},{2,1},{3,0},{4,3},{5,2},{6,5},{7,4},{8,15},{9,14},{10,... | collective-permute-start | bytes 1179656 | tf_op jit(solution)/shard_map/ppermute | solution.py:357
  84.3 17.9 %collective-permute-start = (bf16[512,384]{1,0:T(8,128)(2,1)S(1)}, bf16[512,384]{1,0:T(8,128)(2,1)S(1)}, u32[]{:S(2)}, u32[]{:S(2)}) collective-permute-start(bf16[512,384]{1,0:T(8,128)(2,1)S(1)} %get-tuple-element.18), channel_id=1, source_target_pairs={{0,2},{1,3},{2,4},{3,5},{4,6},{5,7},{6,0},{7,1},{8,10},{9,11},{10,... | collective-permute-start | bytes 1179656 | tf_op jit(solution)/shard_map/ppermute | solution.py:357
  85.4 16.8 %collective-permute-start.1 = (bf16[512,384]{1,0:T(8,128)(2,1)S(1)}, bf16[512,384]{1,0:T(8,128)(2,1)S(1)}, u32[]{:S(2)}, u32[]{:S(2)}) collective-permute-start(bf16[512,384]{1,0:T(8,128)(2,1)S(1)} %get-tuple-element.19), channel_id=1, source_target_pairs={{0,6},{1,7},{2,0},{3,1},{4,2},{5,3},{6,4},{7,5},{8,14},{9,15},{10,... | collective-permute-start | bytes 1179656 | tf_op jit(solution)/shard_map/ppermute | solution.py:357
  86.9 15.2 %all-to-all-start.1 = ((f32[8,1,512]{2,1,0:T(1,128)}), f32[8,1,512]{2,1,0:T(1,128)S(1)}, u32[]{:S(2)}, u32[]{:S(2)}) async-start(f32[8,1,512]{2,1,0:T(1,128)} %get-tuple-element.29), calls=%async_computation.1 | async-start | bytes 32768 | tf_op jit(solution)/shard_map/all_to_all | solution.py:366
